TPU v7x, 32 devices: a whole 2x2x4 slice. The times are simulated.
32 devices in a mesh: dp: 4 (over z), row: 4 (over y, x), col: 2 (over core).
Axes of the slice: x: 2, y: 2, z: 4, core: 2. Of those that a mesh axis runs over, the one named last changes fastest.
Arguments:
- tokens: bfloat16 [16, 2048, 768], P(('dp', 'row'), 'col'), may hold values from -6 to 6
- timesteps: int32 [16], P(('dp', 'row')), may hold values from 0 to 999
- block_ids: int32 [16, 2048], P(('dp', 'row')), may hold values from 0 to 11, never falling along the last dimension, each value on 1 to 256 neighbouring positions
- table: float32 [1000, 768], replicated, may hold values from -3 to 3
- gain_one: float32 [768], replicated, may hold values from 0.5 to 1.5
- bias_one: float32 [768], replicated, may hold values from -1.75 to 1.75
- w_query: float32 [768, 768], P('row', 'col'), may hold values from -0.21875 to 0.21875
- w_key: float32 [768, 768], P('row', 'col'), may hold values from -0.21875 to 0.21875
- w_value: float32 [768, 768], P('row', 'col'), may hold values from -0.21875 to 0.21875
- b_query: float32 [768], P('col'), may hold values from -1.75 to 1.75
- b_value: float32 [768], P('col'), may hold values from -1.75 to 1.75
- w_out: float32 [768, 768], P('col', 'row'), may hold values from -3.5 to 3.5
- b_out: float32 [768], replicated, may hold values from -1.75 to 1.75
- gain_two: float32 [768], replicated, may hold values from 0.5 to 1.5
- bias_two: float32 [768], replicated, may hold values from -1.75 to 1.75
- w_up: float32 [768, 3072], P('row', 'col'), may hold values from -0.21875 to 0.21875
- b_up: float32 [3072], P('col'), may hold values from -1.75 to 1.75
- w_down: float32 [3072, 768], P('col', 'row'), may hold values from -0.109375 to 0.109375
- b_down: float32 [768], replicated, may hold values from -1.75 to 1.75
- cotangent: bfloat16 [16, 2048, 768], P(('dp', 'row'), 'col'), may hold values from -6 to 6
Outputs:
- layer_out: bfloat16 [16, 2048, 768], P(('dp', 'row'), 'col')
- grad_tokens: float32 [16, 2048, 768], P(('dp', 'row'), 'col')
- grad_table: float32 [1000, 768], replicated
- grad_gain_one: float32 [768], replicated
- grad_bias_one: float32 [768], replicated
- grad_w_query: float32 [768, 768], P('row', 'col')
- grad_w_key: float32 [768, 768], P('row', 'col')
- grad_w_value: float32 [768, 768], P('row', 'col')
- grad_b_query: float32 [768], P('col')
- grad_b_value: float32 [768], P('col')
- grad_w_out: float32 [768, 768], P('col', 'row')
- grad_b_out: float32 [768], replicated
- grad_gain_two: float32 [768], replicated
- grad_bias_two: float32 [768], replicated
- grad_w_up: float32 [768, 3072], P('row', 'col')
- grad_b_up: float32 [3072], P('col')
- grad_w_down: float32 [3072, 768], P('col', 'row')
- grad_b_down: float32 [768], replicated
Inputs may be any that keep to these rules, and one draw needn't show every extreme that they name: `block_ids`: block numbers never fall along a sequence; every block number of a sequence is used, each block holds 1 to 256 positions, and some block holds exactly 256.
All inputs are finite; a program needn't handle non-finite values.
Results may differ from a plain program's by a relative error of at most 0.012.
The roundings to bfloat16 on the way count: a program that leaves them out, or rounds other values in their place, can miss the bound.
Values may be sent and summed in bfloat16 or wider, within the bound.
No kernel may reach another device: no remote copies, remote signals or barrier semaphores. Data moves between devices by JAX's collectives and lax.ppermute only.
A program may use at most 256 MiB of HBM per device.

v0:
```python
import jax
import jax.numpy as jnp
from jax import lax
from jax.sharding import PartitionSpec as P

HEAD_DIM = 64


norm_eps = 1e-05
masked_score = -1000000000.0


def layer_norm_parts(values, gain, bias):
    mean = jnp.mean(values, axis=-1, keepdims=True)
    centred = values - mean
    inverse = lax.rsqrt(jnp.mean(centred * centred, axis=-1, keepdims=True) + norm_eps)
    unit = centred * inverse
    return (unit * gain + bias, unit, inverse)


def norm_back(grad_normed, unit, inverse, gain):
    grad_unit = grad_normed * gain
    first_mean = jnp.mean(grad_unit, axis=-1, keepdims=True)
    second_mean = jnp.mean(grad_unit * unit, axis=-1, keepdims=True)
    return inverse * (grad_unit - first_mean - unit * second_mean)


def gelu_exact(values):
    return jax.nn.gelu(values, approximate=False)


def shards(
    tokens,
    timesteps,
    block_ids,
    table,
    gain_one,
    bias_one,
    w_query,
    w_key,
    w_value,
    b_query,
    b_value,
    w_out,
    b_out,
    gain_two,
    bias_two,
    w_up,
    b_up,
    w_down,
    b_down,
    cotangent,
):
    seq_count, local_len, model_width = tokens.shape
    full_len = block_ids.shape[1]
    head_cols = w_query.shape[1]
    hidden_cols = w_up.shape[1]
    local_heads = head_cols // HEAD_DIM
    row_block = min(512, full_len)
    block_count = full_len // row_block
    scale_factor = HEAD_DIM ** (-0.5)
    col_index = lax.axis_index("col")
    row_index = lax.axis_index("row")
    row_size = lax.axis_size("row")
    query_low = w_query.astype(jnp.bfloat16)
    key_low = w_key.astype(jnp.bfloat16)
    value_low = w_value.astype(jnp.bfloat16)
    up_low = w_up.astype(jnp.bfloat16)
    out_low = w_out.astype(jnp.bfloat16)
    down_low = w_down.astype(jnp.bfloat16)
    query_full, key_full, value_full, up_full, out_full, down_full = (
        lax.all_gather(query_low, "row", axis=0, tiled=True),
        lax.all_gather(key_low, "row", axis=0, tiled=True),
        lax.all_gather(value_low, "row", axis=0, tiled=True),
        lax.all_gather(up_low, "row", axis=0, tiled=True),
        lax.all_gather(out_low, "row", axis=1, tiled=True),
        lax.all_gather(down_low, "row", axis=1, tiled=True),
    )
    step_onehot = (
        lax.broadcasted_iota(jnp.int32, (seq_count, table.shape[0]), 1) == timesteps[:, None]
    ).astype(jnp.float32)
    table_rows = jnp.dot(
        step_onehot, table, precision=lax.Precision.HIGHEST, preferred_element_type=jnp.float32
    )
    start = tokens.astype(jnp.float32) + table_rows[:, None, :]
    normed_one, unit_one, inverse_one = layer_norm_parts(start, gain_one, bias_one)
    rows_one = lax.all_gather(normed_one.astype(jnp.bfloat16), "col", axis=1, tiled=True).reshape(
        seq_count * full_len, model_width
    )
    query = (jnp.dot(rows_one, query_full, preferred_element_type=jnp.float32) + b_query).astype(
        jnp.bfloat16
    )
    key = jnp.dot(rows_one, key_full, preferred_element_type=jnp.float32).astype(jnp.bfloat16)
    value = (jnp.dot(rows_one, value_full, preferred_element_type=jnp.float32) + b_value).astype(
        jnp.bfloat16
    )
    query_seq = query.reshape(seq_count, block_count, row_block, local_heads, HEAD_DIM)
    key_seq = key.reshape(seq_count, full_len, local_heads, HEAD_DIM)
    value_seq = value.reshape(seq_count, full_len, local_heads, HEAD_DIM)
    query_ids_all = block_ids.reshape(seq_count, block_count, row_block)

    def scores_for(query_part, key_part, query_ids, key_ids):
        scores = (
            jnp.einsum("qhd,khd->hqk", query_part, key_part, preferred_element_type=jnp.float32)
            * scale_factor
        )
        allowed = key_ids[None, None, :] <= query_ids[None, :, None]
        return jnp.where(allowed, scores, masked_score)

    def forward_seq(pieces):
        query_blocks, key_part, value_part, ids_blocks, key_ids = pieces

        def forward_block(inner):
            query_part, query_ids = inner
            scores = scores_for(query_part, key_part, query_ids, key_ids)
            top = jnp.max(scores, axis=-1, keepdims=True)
            expo = jnp.exp(scores - top)
            total = jnp.sum(expo, axis=-1, keepdims=True)
            probs = (expo / total).astype(jnp.bfloat16)
            mixed = jnp.einsum(
                "hqk,khd->qhd", probs, value_part, preferred_element_type=jnp.float32
            )
            return (mixed, (top + jnp.log(total))[..., 0])

        return lax.map(forward_block, (query_blocks, ids_blocks))

    attended, log_sums = lax.map(
        forward_seq, (query_seq, key_seq, value_seq, query_ids_all, block_ids)
    )
    attended_low = attended.reshape(seq_count * full_len, head_cols).astype(jnp.bfloat16)
    branch_part = jnp.dot(attended_low, out_full, preferred_element_type=jnp.float32).reshape(
        seq_count, full_len, model_width
    )
    branch = lax.psum_scatter(branch_part, "col", scatter_dimension=1, tiled=True)
    middle = start + branch + b_out
    normed_two, unit_two, inverse_two = layer_norm_parts(middle, gain_two, bias_two)
    rows_two = lax.all_gather(normed_two.astype(jnp.bfloat16), "col", axis=1, tiled=True).reshape(
        seq_count * full_len, model_width
    )
    hidden_pre = jnp.dot(rows_two, up_full, preferred_element_type=jnp.float32) + b_up
    hidden_low = gelu_exact(hidden_pre).astype(jnp.bfloat16)
    mixer_part = jnp.dot(hidden_low, down_full, preferred_element_type=jnp.float32).reshape(
        seq_count, full_len, model_width
    )
    mixer = lax.psum_scatter(
        mixer_part.astype(jnp.bfloat16), "col", scatter_dimension=1, tiled=True
    ).astype(jnp.float32)
    layer_out = (middle + mixer + b_down).astype(jnp.bfloat16)
    grad_out = cotangent.astype(jnp.float32)
    grad_mixer_rows = lax.all_gather(cotangent, "col", axis=1, tiled=True).reshape(
        seq_count * full_len, model_width
    )
    grad_b_down = jnp.sum(cotangent, axis=(0, 1), dtype=jnp.float32)
    grad_down = jnp.einsum(
        "rf,rd->fd", hidden_low, grad_mixer_rows, preferred_element_type=jnp.float32
    )
    grad_hidden = jnp.einsum(
        "rd,fd->rf", grad_mixer_rows, down_full, preferred_element_type=jnp.float32
    )
    grad_pre = jax.vjp(gelu_exact, hidden_pre)[1](grad_hidden)[0]
    grad_pre_low = grad_pre.astype(jnp.bfloat16)
    grad_up = jnp.einsum("rd,rf->df", rows_two, grad_pre_low, preferred_element_type=jnp.float32)
    grad_b_up_local = jnp.sum(grad_pre_low, axis=0, dtype=jnp.float32)
    grad_normed_two_part = jnp.einsum(
        "rf,df->rd", grad_pre_low, up_full, preferred_element_type=jnp.float32
    ).reshape(seq_count, full_len, model_width)
    grad_normed_two = lax.psum_scatter(grad_normed_two_part, "col", scatter_dimension=1, tiled=True)
    grad_gain_two = jnp.sum(grad_normed_two * unit_two, axis=(0, 1))
    grad_bias_two = jnp.sum(grad_normed_two, axis=(0, 1))
    grad_middle = grad_out + norm_back(grad_normed_two, unit_two, inverse_two, gain_two)
    grad_branch_low = grad_middle.astype(jnp.bfloat16)
    grad_b_out = jnp.sum(grad_branch_low, axis=(0, 1), dtype=jnp.float32)
    grad_branch_rows = lax.all_gather(grad_branch_low, "col", axis=1, tiled=True).reshape(
        seq_count * full_len, model_width
    )
    grad_out_proj = jnp.einsum(
        "rh,rd->hd", attended_low, grad_branch_rows, preferred_element_type=jnp.float32
    )
    grad_attended = jnp.einsum(
        "rd,hd->rh", grad_branch_rows, out_full, preferred_element_type=jnp.float32
    ).astype(jnp.bfloat16)
    grad_att_seq = grad_attended.reshape(seq_count, block_count, row_block, local_heads, HEAD_DIM)

    def backward_seq(pieces):
        query_blocks, key_part, value_part, ids_blocks, key_ids, grad_blocks, sums_blocks = pieces

        def backward_block(carry, inner):
            query_part, query_ids, grad_part, log_part = inner
            scores = scores_for(query_part, key_part, query_ids, key_ids)
            probs = jnp.exp(scores - log_part[:, :, None])
            grad_probs = jnp.einsum(
                "qhd,khd->hqk", grad_part, value_part, preferred_element_type=jnp.float32
            )
            inner_sum = jnp.sum(probs * grad_probs, axis=-1, keepdims=True)
            grad_scores = (probs * (grad_probs - inner_sum)).astype(jnp.bfloat16)
            grad_query_part = (
                jnp.einsum(
                    "hqk,khd->qhd", grad_scores, key_part, preferred_element_type=jnp.float32
                )
                * scale_factor
            )
            key_acc = (
                carry[0]
                + jnp.einsum(
                    "hqk,qhd->khd", grad_scores, query_part, preferred_element_type=jnp.float32
                )
                * scale_factor
            )
            value_acc = carry[1] + jnp.einsum(
                "hqk,qhd->khd",
                probs.astype(jnp.bfloat16),
                grad_part,
                preferred_element_type=jnp.float32,
            )
            return ((key_acc, value_acc), grad_query_part)

        empty = jnp.zeros((full_len, local_heads, HEAD_DIM), jnp.float32)
        (grad_key_part, grad_value_part), grad_query_blocks = lax.scan(
            backward_block, (empty, empty), (query_blocks, ids_blocks, grad_blocks, sums_blocks)
        )
        return (grad_query_blocks, grad_key_part, grad_value_part)

    grad_query_all, grad_key_all, grad_value_all = lax.map(
        backward_seq,
        (query_seq, key_seq, value_seq, query_ids_all, block_ids, grad_att_seq, log_sums),
    )
    grad_query_low = grad_query_all.reshape(seq_count * full_len, head_cols).astype(jnp.bfloat16)
    grad_key_low = grad_key_all.reshape(seq_count * full_len, head_cols).astype(jnp.bfloat16)
    grad_value_low = grad_value_all.reshape(seq_count * full_len, head_cols).astype(jnp.bfloat16)
    grad_w_query = jnp.einsum(
        "rd,rh->dh", rows_one, grad_query_low, preferred_element_type=jnp.float32
    )
    grad_w_key = jnp.einsum("rd,rh->dh", rows_one, grad_key_low, preferred_element_type=jnp.float32)
    grad_w_value = jnp.einsum(
        "rd,rh->dh", rows_one, grad_value_low, preferred_element_type=jnp.float32
    )
    grad_b_query_local = jnp.sum(grad_query_low, axis=0, dtype=jnp.float32)
    grad_b_value_local = jnp.sum(grad_value_low, axis=0, dtype=jnp.float32)
    grad_normed_one_part = (
        jnp.einsum("rh,dh->rd", grad_query_low, query_full, preferred_element_type=jnp.float32)
        + jnp.einsum("rh,dh->rd", grad_key_low, key_full, preferred_element_type=jnp.float32)
        + jnp.einsum("rh,dh->rd", grad_value_low, value_full, preferred_element_type=jnp.float32)
    ).reshape(seq_count, full_len, model_width)
    grad_normed_one = lax.psum_scatter(grad_normed_one_part, "col", scatter_dimension=1, tiled=True)
    grad_gain_one = jnp.sum(grad_normed_one * unit_one, axis=(0, 1))
    grad_bias_one = jnp.sum(grad_normed_one, axis=(0, 1))
    grad_tokens = grad_middle + norm_back(grad_normed_one, unit_one, inverse_one, gain_one)
    token_sums = jnp.sum(grad_tokens, axis=1)

    def widen(local_vec, full_size):
        return lax.dynamic_update_slice_in_dim(
            jnp.zeros((full_size,), jnp.float32), local_vec, col_index * local_vec.shape[0], 0
        )

    wide_query_bias = widen(grad_b_query_local, model_width)
    wide_value_bias = widen(grad_b_value_local, model_width)
    wide_up_bias = widen(grad_b_up_local, hidden_cols * lax.axis_size("col"))
    grad_table = jnp.einsum(
        "sv,sd->vd",
        step_onehot,
        token_sums,
        precision=lax.Precision.HIGHEST,
        preferred_element_type=jnp.float32,
    )
    (
        sum_table,
        sum_gain_one,
        sum_bias_one,
        sum_query_bias,
        sum_value_bias,
        sum_out_bias,
        sum_gain_two,
        sum_bias_two,
        sum_up_bias,
        sum_down_bias,
    ) = lax.psum(
        (
            grad_table,
            grad_gain_one,
            grad_bias_one,
            wide_query_bias,
            wide_value_bias,
            grad_b_out,
            grad_gain_two,
            grad_bias_two,
            wide_up_bias,
            grad_b_down,
        ),
        ("dp", "row", "col"),
    )
    grad_b_query = lax.dynamic_slice_in_dim(sum_query_bias, col_index * head_cols, head_cols, 0)
    grad_b_value = lax.dynamic_slice_in_dim(sum_value_bias, col_index * head_cols, head_cols, 0)
    grad_b_up = lax.dynamic_slice_in_dim(sum_up_bias, col_index * hidden_cols, hidden_cols, 0)

    def owned_rows(grad_whole, dim_pick):
        share = grad_whole.shape[dim_pick] // row_size
        return lax.dynamic_slice_in_dim(grad_whole, row_index * share, share, dim_pick)

    summed = lax.psum(
        (grad_w_query, grad_w_key, grad_w_value, grad_up, grad_out_proj, grad_down), ("dp", "row")
    )
    owned_query = owned_rows(summed[0], 0)
    owned_key = owned_rows(summed[1], 0)
    owned_value = owned_rows(summed[2], 0)
    owned_up = owned_rows(summed[3], 0)
    owned_out = owned_rows(summed[4], 1)
    owned_down = owned_rows(summed[5], 1)
    return (
        layer_out,
        grad_tokens,
        sum_table,
        sum_gain_one,
        sum_bias_one,
        owned_query,
        owned_key,
        owned_value,
        grad_b_query,
        grad_b_value,
        owned_out,
        sum_out_bias,
        sum_gain_two,
        sum_bias_two,
        owned_up,
        grad_b_up,
        owned_down,
        sum_down_bias,
    )


def solution(mesh):
    return jax.shard_map(
        shards,
        mesh=mesh,
        in_specs=(
            P(("dp", "row"), "col", None),
            P(("dp", "row")),
            P(("dp", "row"), None),
            P(),
            P(),
            P(),
            P("row", "col"),
            P("row", "col"),
            P("row", "col"),
            P("col"),
            P("col"),
            P("col", "row"),
            P(),
            P(),
            P(),
            P("row", "col"),
            P("col"),
            P("col", "row"),
            P(),
            P(("dp", "row"), "col", None),
        ),
        out_specs=(
            P(("dp", "row"), "col", None),
            P(("dp", "row"), "col", None),
            P(),
            P(),
            P(),
            P("row", "col"),
            P("row", "col"),
            P("row", "col"),
            P("col"),
            P("col"),
            P("col", "row"),
            P(),
            P(),
            P(),
            P("row", "col"),
            P("col"),
            P("col", "row"),
            P(),
        ),
        check_vma=False,
    )
```

profile of v0, /device:TPU:0, one launch (start us, length us, event | category | flops | bytes accessed | tf_op | source)
XLA Modules:
  0.0 1383.5 jit_solution(9425003297407014153)
XLA Ops:
  16.0 12.7 all_gather.34
  28.7 11.2 all_gather.33
  39.9 10.9 all_gather.32
  50.8 10.1 all_gather.31
  81.4 149.2 %while.47 = (s32[]{:T(128)}, bf16[4,512,6,64]{1,3,2,0:T(8,128)(2,1)}, f32[4,6,512]{2,1,0:T(8,128)}, s32[2048]{0:T(1024)S(1)}, s32[4,512]{1,0:T(4,128)S(1)}, /*in...) while((s32[]{:T(128)}, ...), condition=%wide.region_5.6_spmd, body=%wide.region_2.5_spmd.sunk | while | flops 1687155712 | bytes 103016640 | solution.py:125
  82.0 11.6 fusion.135
  93.7 12.1 fusion.136
  105.8 11.6 fusion.137
  119.2 11.6 fusion.135
  130.9 12.1 fusion.136
  143.0 11.6 fusion.137
  156.4 11.6 fusion.135
  168.1 12.1 fusion.136
  180.2 11.6 fusion.137
  193.6 11.6 fusion.135
  205.3 12.1 fusion.136
  217.4 11.6 fusion.137
  242.2 12.7 reduce-scatter.5.cloned.1.call-done
  262.4 18.1 %all-gather.11.cloned.1.call-done = bf16[768,1536]{1,0:T(8,128)(2,1)} async-done(((bf16[192,1536]{1,0:T(8,128)(2,1)}), bf16[768,1536]{1,0:T(8,128)(2,1)}) %all-gather.11.cloned.1.call-update) | async-done | bytes 2359312 | tf_op jit(solution)/shard_map/all_gather | solution.py:75
  280.5 14.1 %all-gather.9.cloned.1.call-done = bf16[1,2048,768]{2,1,0:T(8,128)(2,1)} async-done(((bf16[1,1024,768]{2,1,0:T(8,128)(2,1)}), bf16[1,2048,768]{2,1,0:T(8,128)(2,1)}) %all-gather.9.cloned.1.call-update) | async-done | bytes 3145744 | tf_op jit(solution)/shard_map/all_gather | solution.py:137
  294.6 34.8 %multiply_convert_fusion.1 = (bf16[2048,1536]{1,0:T(8,128)(2,1)}, f32[2048,1536]{1,0:T(8,128)}, f32[2048,1536]{1,0:T(8,128)}) fusion(f32[1536]{0:T(1024)S(1)} %copy-done.70, bf16[768,1536]{1,0:T(8,128)(2,1)} %all-gather.11.cloned.1.call-done, bf16[1,2048,768]{2,1,0:T(8,128)(2,1)} %all-gather.9.cloned.1.call-done), kind=kOutput, calls=%fused_computation.51 | convolution fusion | flops 5039456256 | bytes 36968448 | tf_op jit(solution)/shard_map/dot_general | solution.py:140
  329.4 21.0 %all-gather.13.cloned.1.call-done = bf16[1536,768]{0,1:T(8,128)(2,1)} async-done(((bf16[1536,192]{0,1:T(8,128)(2,1)}), bf16[1536,768]{0,1:T(8,128)(2,1)}) %all-gather.13.cloned.1.call-update) | async-done | bytes 2359312 | tf_op jit(solution)/shard_map/all_gather | solution.py:77
  350.4 17.7 %convert_reduce_fusion = (f32[1536]{0:T(1024)}, bf16[2048,1536]{1,0:T(8,128)(2,1)S(1)}) fusion(f32[2048,1536]{1,0:T(8,128)} %get-tuple-element.325, bf16[1536,768]{0,1:T(8,128)(2,1)} %all-gather.13.cloned.1.call-done, bf16[1,2048,768]{2,1,0:T(8,128)(2,1)} %all-gather.15.cloned.1.call-done, f32[2048,1536]{1,0:T(8,128)} %get-tuple-element.334, ...), kind=kOutput, calls=%fused_computation.49 | convolution fusion | flops 4885314048 | bytes 36974592 | tf_op jit(solution)/shard_map/rd,fd->rf/dot_general | solution.py:157
  396.4 10.1 reduce-scatter.7.cloned.1.call-done
  413.0 13.5 all-gather.17.cloned.1.call-done
  439.8 339.8 %while.48 = (s32[]{:T(128)}, f32[2048,6,64]{0,2,1:T(8,128)}, f32[2048,6,64]{0,2,1:T(8,128)}, bf16[4,512,6,64]{1,3,2,0:T(8,128)(2,1)}, bf16[4,512,6,64]{1,3,2,0:T...) while((s32[]{:T(128)}, f32[2048,6,64]{0,2,1:T(8,128)}, ...), condition=%wide.region_15.16_spmd.clone, body=%wide.region_13.15_spmd.clone.sunk | while | flops 4126077952 | bytes 212699312 | solution.py:218
  442.3 11.2 fusion.147
  453.5 12.9 bitcast_add_fusion.5
  466.4 18.1 %multiply_reduce_fusion.10 = (f32[6,512]{1,0:T(8,128)S(1)}, f32[6,512,2048]{2,1,0:T(8,128)}) fusion(f32[6,512,2048]{2,1,0:T(8,128)} %fusion.147, f32[6,512]{1,0:T(8,128)S(1)} %dynamic-slice_bitcast_fusion.2, pred[512,2048]{1,0:T(8,128)(4,1)S(1)} %broadcast_compare_fusion.5, bf16[2048,6,64]{0,2,1:T(8,128)(2,1)} %get-tuple-element.526, ...), kind=kOutput, calls=%fused_computation.18.clone.1 | convolution fusion | flops 836760576 | bytes 53370884 | tf_op jit(solution)/shard_map/while/body/eval_jaxpr/while/body/eval_jaxpr/qhd,khd->hqk/dot_general | solution.py:191
  484.5 21.3 %multiply_convert_fusion.3 = bf16[6,512,2048]{2,1,0:T(8,128)(2,1)} fusion(f32[6,512,2048]{2,1,0:T(8,128)} %get-tuple-element.461, f32[6,512,2048]{2,1,0:T(8,128)} %fusion.147, f32[6,512]{1,0:T(8,128)S(1)} %get-tuple-element.462, f32[6,512]{1,0:T(8,128)S(1)} %dynamic-slice_bitcast_fusion.2, pred[512,2048]{1,0:T(8,128)(4,1)S(1)} %broadcast_compare_fusion.5), kind=kLoop, calls=%fused_computation.17.clone.1 | loop fusion | flops 37748736 | bytes 63987712 | tf_op jit(solution)/shard_map/while/body/eval_jaxpr/while/body/eval_jaxpr/convert_element_type | solution.py:195
  525.7 11.2 fusion.147
  536.9 13.8 bitcast_add_fusion.5
  550.7 18.1 %multiply_reduce_fusion.10 = (f32[6,512]{1,0:T(8,128)S(1)}, f32[6,512,2048]{2,1,0:T(8,128)}) fusion(f32[6,512,2048]{2,1,0:T(8,128)} %fusion.147, f32[6,512]{1,0:T(8,128)S(1)} %dynamic-slice_bitcast_fusion.2, pred[512,2048]{1,0:T(8,128)(4,1)S(1)} %broadcast_compare_fusion.5, bf16[2048,6,64]{0,2,1:T(8,128)(2,1)} %get-tuple-element.526, ...), kind=kOutput, calls=%fused_computation.18.clone.1 | convolution fusion | flops 836760576 | bytes 53370884 | tf_op jit(solution)/shard_map/while/body/eval_jaxpr/while/body/eval_jaxpr/qhd,khd->hqk/dot_general | solution.py:191
  568.8 21.3 %multiply_convert_fusion.3 = bf16[6,512,2048]{2,1,0:T(8,128)(2,1)} fusion(f32[6,512,2048]{2,1,0:T(8,128)} %get-tuple-element.461, f32[6,512,2048]{2,1,0:T(8,128)} %fusion.147, f32[6,512]{1,0:T(8,128)S(1)} %get-tuple-element.462, f32[6,512]{1,0:T(8,128)S(1)} %dynamic-slice_bitcast_fusion.2, pred[512,2048]{1,0:T(8,128)(4,1)S(1)} %broadcast_compare_fusion.5), kind=kLoop, calls=%fused_computation.17.clone.1 | loop fusion | flops 37748736 | bytes 63987712 | tf_op jit(solution)/shard_map/while/body/eval_jaxpr/while/body/eval_jaxpr/convert_element_type | solution.py:195
  599.3 9.6 bitcast_add_fusion.4
  611.0 11.2 fusion.147
  622.2 13.8 bitcast_add_fusion.5
  636.0 18.1 %multiply_reduce_fusion.10 = (f32[6,512]{1,0:T(8,128)S(1)}, f32[6,512,2048]{2,1,0:T(8,128)}) fusion(f32[6,512,2048]{2,1,0:T(8,128)} %fusion.147, f32[6,512]{1,0:T(8,128)S(1)} %dynamic-slice_bitcast_fusion.2, pred[512,2048]{1,0:T(8,128)(4,1)S(1)} %broadcast_compare_fusion.5, bf16[2048,6,64]{0,2,1:T(8,128)(2,1)} %get-tuple-element.526, ...), kind=kOutput, calls=%fused_computation.18.clone.1 | convolution fusion | flops 836760576 | bytes 53370884 | tf_op jit(solution)/shard_map/while/body/eval_jaxpr/while/body/eval_jaxpr/qhd,khd->hqk/dot_general | solution.py:191
  654.1 21.3 %multiply_convert_fusion.3 = bf16[6,512,2048]{2,1,0:T(8,128)(2,1)} fusion(f32[6,512,2048]{2,1,0:T(8,128)} %get-tuple-element.461, f32[6,512,2048]{2,1,0:T(8,128)} %fusion.147, f32[6,512]{1,0:T(8,128)S(1)} %get-tuple-element.462, f32[6,512]{1,0:T(8,128)S(1)} %dynamic-slice_bitcast_fusion.2, pred[512,2048]{1,0:T(8,128)(4,1)S(1)} %broadcast_compare_fusion.5), kind=kLoop, calls=%fused_computation.17.clone.1 | loop fusion | flops 37748736 | bytes 63987712 | tf_op jit(solution)/shard_map/while/body/eval_jaxpr/while/body/eval_jaxpr/convert_element_type | solution.py:195
  696.3 11.2 fusion.147
  707.5 13.8 bitcast_add_fusion.5
  721.3 18.1 %multiply_reduce_fusion.10 = (f32[6,512]{1,0:T(8,128)S(1)}, f32[6,512,2048]{2,1,0:T(8,128)}) fusion(f32[6,512,2048]{2,1,0:T(8,128)} %fusion.147, f32[6,512]{1,0:T(8,128)S(1)} %dynamic-slice_bitcast_fusion.2, pred[512,2048]{1,0:T(8,128)(4,1)S(1)} %broadcast_compare_fusion.5, bf16[2048,6,64]{0,2,1:T(8,128)(2,1)} %get-tuple-element.526, ...), kind=kOutput, calls=%fused_computation.18.clone.1 | convolution fusion | flops 836760576 | bytes 53370884 | tf_op jit(solution)/shard_map/while/body/eval_jaxpr/while/body/eval_jaxpr/qhd,khd->hqk/dot_general | solution.py:191
  739.4 21.3 %multiply_convert_fusion.3 = bf16[6,512,2048]{2,1,0:T(8,128)(2,1)} fusion(f32[6,512,2048]{2,1,0:T(8,128)} %get-tuple-element.461, f32[6,512,2048]{2,1,0:T(8,128)} %fusion.147, f32[6,512]{1,0:T(8,128)S(1)} %get-tuple-element.462, f32[6,512]{1,0:T(8,128)S(1)} %dynamic-slice_bitcast_fusion.2, pred[512,2048]{1,0:T(8,128)(4,1)S(1)} %broadcast_compare_fusion.5), kind=kLoop, calls=%fused_computation.17.clone.1 | loop fusion | flops 37748736 | bytes 63987712 | tf_op jit(solution)/shard_map/while/body/eval_jaxpr/while/body/eval_jaxpr/convert_element_type | solution.py:195
  794.7 9.8 fusion.48
  804.6 11.0 fusion.45
  839.1 46.3 %all-reduce = (f32[768]{0:T(1024)}, f32[768]{0:T(1024)}, f32[768]{0:T(1024)S(1)}, f32[768]{0:T(1024)S(1)}, f32[768]{0:T(1024)}, /*index=5*/f32[768]{0:T(1024)}, f32[768]{0:T(1024)}, f32[3072]{0:T(1024)S(1)}, f32[768]{0:T(1024)}) all-reduce(f32[768]{0:T(1024)S(1)} %get-tuple-element.258, ...), channel_id=1, replica_groups=mesh['dp'=4,'row'=4,'col'=2] {'dp','row','col'}, use_global_device_ids=true, to_apply=%region_22.23 | all-reduce | flops 9216 | bytes 73728 | tf_op jit(solution)/shard_map/psum | solution.py:276
  887.4 341.9 %all-reduce.7.cloned.1.call-done = (f32[768,384]{1,0:T(8,128)}, f32[768,384]{1,0:T(8,128)}, f32[768,384]{1,0:T(8,128)}, f32[384,768]{0,1:T(8,128)}, f32[768,1536]{1,0:T(8,128)}, /*index=5*/f32[1536,768]{0,1:T(8,128)}) async-done(((f32[768,384]{1,0:T(8,128)}, f32[768,384]{1,0:T(8,128)}, f32[768,384]{1,0:T(8,128)}, f32[384,768]{0,1:T(8,128)}, f32[768,1536]{1,0:T(8,128)}, /*index=5*/f32[1536,768]{0,1:T(8,128)}), ...) | async-done | bytes 14155792 | tf_op jit(solution)/shard_map/psum | solution.py:299
  1240.9 131.2 %all-reduce.5.cloned.1.call-done = f32[1000,768]{1,0:T(8,128)} async-done(((f32[1000,768]{1,0:T(8,128)}), f32[1000,768]{1,0:T(8,128)}) %all-reduce.5.cloned.1.call-update) | async-done | bytes 3072016 | tf_op jit(solution)/shard_map/psum | solution.py:276
  (306 shorter events, 230.3 us)
Async XLA Ops:
  8.0 4.7 copy-start.51
  8.1 4.7 copy-start.60
  8.1 52.9 %all-gather.7.cloned.1.call-start = ((), (), s32[]{:S(2)}) async-start(), calls=%async_computation.4 | async-start | bytes 4718592 | tf_op jit(solution)/shard_map/all_gather | solution.py:87
  12.0 3.9 copy-start.35
  12.0 4.0 copy-start.36
  14.6 47.2 %copy-start.71 = (f32[384]{0:T(512)S(1)}, f32[384]{0:T(512)}, u32[]{:S(2)}) copy-start(f32[384]{0:T(512)} %param.33) | copy-start | bytes 4612
  14.6 240.3 %reduce-scatter.5.cloned.1.call-start = ((), (), s32[]{:S(2)}) async-start(), calls=%async_computation.5 | async-start | bytes 9437184 | tf_op jit(solution)/shard_map/reduce_scatter | solution.py:134
  73.8 3.5 copy-start.64
  73.8 3.5 copy-start.72
  93.7 12.1 copy-start.8
  93.7 12.1 copy-start.20
  130.9 12.1 copy-start.8
  130.9 12.1 copy-start.20
  168.1 12.1 copy-start.8
  168.1 12.1 copy-start.20
  205.3 12.1 copy-start.8
  205.3 12.1 copy-start.20
  230.6 3.7 copy-start.2
  230.6 3.7 copy-start.46
  230.6 4.9 copy-start.29
  239.9 14.9 %copy-start.6 = (bf16[1,1024,768]{2,1,0:T(8,128)(2,1)S(1)}, bf16[1,1024,768]{2,1,0:T(8,128)(2,1)}, u32[]{:S(2)}) copy-start(bf16[1,1024,768]{2,1,0:T(8,128)(2,1)} %param.24) | copy-start | bytes 4718596
  239.9 14.9 %copy-start.40 = (f32[768]{0:T(1024)S(1)}, f32[768]{0:T(1024)}, u32[]{:S(2)}) copy-start(f32[768]{0:T(1024)} %copy-done.39) | copy-start | bytes 9220
  239.9 14.9 %copy-start.61 = (f32[768]{0:T(1024)S(1)}, f32[768]{0:T(1024)}, u32[]{:S(2)}) copy-start(f32[768]{0:T(1024)} %param.36) | copy-start | bytes 9220
  240.0 40.5 %all-gather.11.cloned.1.call-start = ((), (), s32[]{:S(2)}) async-start(), calls=%async_computation.7 | async-start | bytes 2949120 | tf_op jit(solution)/shard_map/all_gather | solution.py:75
  242.1 52.5 %all-gather.9.cloned.1.call-start = ((), (), s32[]{:S(2)}) async-start(), calls=%async_computation.6 | async-start | bytes 4718592 | tf_op jit(solution)/shard_map/all_gather | solution.py:137
  260.7 33.8 %copy-start.70 = (f32[1536]{0:T(1024)S(1)}, f32[1536]{0:T(1024)}, u32[]{:S(2)}) copy-start(f32[1536]{0:T(1024)} %param.40) | copy-start | bytes 18436
  260.8 68.6 %all-gather.15.cloned.1.call-start = ((), (), s32[]{:S(2)}) async-start(), calls=%async_computation.10 | async-start | bytes 4718592 | tf_op jit(solution)/shard_map/all_gather | solution.py:150
  261.4 89.0 %all-gather.13.cloned.1.call-start = ((), (), s32[]{:S(2)}) async-start(), calls=%async_computation.8 | async-start | bytes 2949120 | tf_op jit(solution)/shard_map/all_gather | solution.py:77
  262.3 129.9 %reduce-scatter.9.cloned.1.call-start = ((), (), s32[]{:S(2)}) async-start(), calls=%async_computation.11 | async-start | bytes 9437184 | tf_op jit(solution)/shard_map/reduce_scatter | solution.py:167
  350.4 20.3 %copy-start.68 = (bf16[768,1536]{1,0:T(8,128)(2,1)S(1)}, bf16[768,1536]{1,0:T(8,128)(2,1)}, u32[]{:S(2)}) copy-start(bf16[768,1536]{1,0:T(8,128)(2,1)} %all-gather.11.cloned.1.call-done) | copy-start | bytes 7077892
  377.7 28.7 %reduce-scatter.7.cloned.1.call-start = ((), (), s32[]{:S(2)}) async-start(), calls=%async_computation.9 | async-start | bytes 4718592 | tf_op jit(solution)/shard_map/reduce_scatter | solution.py:145
  388.8 17.7 %copy-start.22 = (bf16[1,1024,768]{2,1,0:T(8,128)(2,1)S(1)}, bf16[1,1024,768]{2,1,0:T(8,128)(2,1)}, u32[]{:S(2)}) copy-start(bf16[1,1024,768]{2,1,0:T(8,128)(2,1)} %param.43) | copy-start | bytes 4718596
  388.8 17.6 %copy-start.63 = (f32[768]{0:T(1024)S(1)}, f32[768]{0:T(1024)}, u32[]{:S(2)}) copy-start(f32[768]{0:T(1024)} %param.42) | copy-start | bytes 9220
  388.9 37.6 %all-gather.17.cloned.1.call-start = ((), (), s32[]{:S(2)}) async-start(), calls=%async_computation.12 | async-start | bytes 4718592 | tf_op jit(solution)/shard_map/all_gather | solution.py:173
  406.5 20.0 %copy-start.30 = (bf16[384,768]{0,1:T(8,128)(2,1)S(1)}, bf16[384,768]{0,1:T(8,128)(2,1)}, u32[]{:S(2)}) copy-start(bf16[384,768]{0,1:T(8,128)(2,1)} %all_gather.34) | copy-start | bytes 1769476
  413.0 414.2 %reduce-scatter.11.cloned.1.call-start = ((), (), s32[]{:S(2)}) async-start(), calls=%async_computation.13 | async-start | bytes 9437184 | tf_op jit(solution)/shard_map/reduce_scatter | solution.py:244
  435.4 4.4 copy-start.3
  435.4 4.4 copy-start.34
  781.9 4.5 copy-start.14
  783.6 4.6 copy-start.16
  786.4 3.8 copy-start.18
  794.7 434.6 %all-reduce.7.cloned.1.call-start = ((), (), s32[]{:S(2)}) async-start(), calls=%async_computation.15 | async-start | bytes 28311552 | tf_op jit(solution)/shard_map/psum | solution.py:299
  794.7 9.8 copy-start.66
  804.6 11.0 copy-start.13
  804.6 11.0 copy-start.67
  827.1 545.0 %all-reduce.5.cloned.1.call-start = ((), (), s32[]{:S(2)}) async-start(), calls=%async_computation.14 | async-start | bytes 6144000 | tf_op jit(solution)/shard_map/psum | solution.py:276
  828.5 3.6 copy-start.11
  1238.4 137.4 %copy-start.1 = (f32[1000,768]{1,0:T(8,128)S(1)}, f32[1000,768]{1,0:T(8,128)}, u32[]{:S(2)}) copy-start(f32[1000,768]{1,0:T(8,128)} %param.27) | copy-start | bytes 9216004
  (47 other events, 100.5 us)
Sparse Core Ops, SparseCore 0:
  14.7 14.8 all-gather.6
  240.1 14.7 reduce-scatter.4
  413.1 13.3 all-gather.16
  794.8 15.6 reduce-scatter.10
  827.2 402.0 all-reduce.6
  1236.1 135.9 all-reduce.4
Sparse Core Ops, SparseCore 1:
  242.9 37.5 all-gather.10
  282.5 12.0 all-gather.8
  296.0 13.2 all-gather.14
  311.9 38.5 all-gather.12
  377.8 14.3 reduce-scatter.8
  394.5 12.0 reduce-scatter.6
where the time goes:
time: 1390 us; the launch traced here: 1380 us
  waiting for transfers between devices  567 us (41%)
  matrix products  470 us (34%)
  other arithmetic  177 us (13%)
  blocking collectives  91.2 us (7%)
  local copies, waits for them, and re-layouts  60.1 us (4%)
  between operations  17.5 us (1%)
    psum x1, waiting for transfers between devices, shards(): lax.psum((grad_w_query, grad_w_key, grad_w_value, grad_up, grad_out_proj,...  342 us
    psum x1, waiting for transfers between devices, shards(): lax.psum((grad_table, grad_gain_one, grad_bias_one, wide_query_bias, wide...  131 us
    dot_general x8, matrix products, scores_for(): jnp.einsum('qhd,khd->hqk', query_part, key_part, preferred_element_type=j...  91.3 us
    convert_element_type x4, other arithmetic, backward_block(): grad_scores = (probs * (grad_probs - inner_sum)).astype(jnp.bfloat16)  85 us
    dot_general x4, matrix products, backward_block(): jnp.einsum('qhd,khd->hqk', grad_part, value_part, preferred_element_type=...  72.5 us
    dot_general x4, matrix products, backward_block(): jnp.einsum('hqk,qhd->khd', probs.astype(jnp.bfloat16), grad_part, preferr...  54.3 us
    reduce_sum x4, other arithmetic, forward_block(): total = jnp.sum(expo, axis=-1, keepdims=True)  48.3 us
    dot_general x4, matrix products, forward_block(): jnp.einsum('hqk,khd->qhd', probs, value_part, preferred_element_type=jnp....  46.5 us
  transfers between devices with their start and end apart: 12, of which 9 were waited for; matrix products, arithmetic and copies ran while one was open for 8% of the time, Pallas kernels for 0%

commit v1 on v0

v1 whole, which is shorter than its diff:
```python
import functools

import jax
import jax.numpy as jnp
from jax import lax
from jax.experimental import pallas as pl
from jax.experimental.pallas import tpu as pltpu
from jax.sharding import PartitionSpec as P

HEAD_DIM = 64
norm_eps = 1e-05
masked_score = -1000000000.0
low = jnp.bfloat16
wide = jnp.float32
tile_rows = 256


def dot_nn(left, right):
    return lax.dot_general(left, right, (((1,), (0,)), ((), ())), preferred_element_type=wide)


def dot_nt(left, right):
    return lax.dot_general(left, right, (((1,), (1,)), ((), ())), preferred_element_type=wide)


def dot_tn(left, right):
    return lax.dot_general(left, right, (((0,), (0,)), ((), ())), preferred_element_type=wide)


def fold_lanes(values, op):
    folded = values[:, :128]
    for start in range(128, values.shape[1], 128):
        folded = op(folded, values[:, start : start + 128])
    return folded


def column_of(ids_row):
    parts = []
    for start in range(0, ids_row.shape[1], 128):
        piece = ids_row[:, start : start + 128].astype(wide)
        parts.append(jnp.transpose(jnp.broadcast_to(piece, (128, 128))))
    return jnp.concatenate(parts, axis=0)


def allowed_mask(ids_ref, ids_column, start, size):
    parts = []
    for lane in range(start, start + size, 128):
        parts.append(ids_ref[:, lane : lane + 128].astype(wide) <= ids_column)
    return jnp.concatenate(parts, axis=1)


def attend_forward_body(count, half, col_ref, q_ref, k_ref, v_ref, ids_ref, o_ref, lse_ref, s_ref):
    step = pl.program_id(1)
    side = col_ref[0]
    size = tile_rows
    lane = lax.broadcasted_iota(jnp.int32, (size, 128), 1)

    def key_tile(ref, j):
        return ref[(j // half) ^ side, (j % half) * size : (j % half + 1) * size, :]

    def variant(c):
        keys = min(c + 2, count)
        query = q_ref[...]
        ids_column = column_of(ids_ref[:, c * size : (c + 1) * size])
        out = None
        for head in range(2):
            mine = (lane < HEAD_DIM) if head == 0 else (lane >= HEAD_DIM)
            part = jnp.where(mine, query, jnp.zeros_like(query)) * jnp.asarray(0.125, low)
            top = None
            for j in range(keys):
                scores = dot_nt(part, key_tile(k_ref, j))
                if j >= c:
                    mask = allowed_mask(ids_ref, ids_column, j * size, size)
                    scores = jnp.where(mask, scores, masked_score)
                s_ref[head, :, j * size : (j + 1) * size] = scores
                peak = fold_lanes(scores, jnp.maximum)
                top = peak if top is None else jnp.maximum(top, peak)
            top = jnp.max(top, axis=1, keepdims=True)
            total = None
            acc = None
            for j in range(keys):
                expo = jnp.exp(s_ref[head, :, j * size : (j + 1) * size] - top)
                part_sum = fold_lanes(expo, jnp.add)
                total = part_sum if total is None else total + part_sum
                mixed = dot_nn(expo.astype(low), key_tile(v_ref, j))
                acc = mixed if acc is None else acc + mixed
            total = jnp.sum(total, axis=1, keepdims=True)
            mixed = acc / total
            out = mixed if head == 0 else jnp.where(mine, mixed, out)
            lse_ref[:, head : head + 1] = top + jnp.log(total)
        o_ref[...] = out.astype(low)

    for c in range(count):
        pl.when(step == c)(functools.partial(variant, c))


def attend_forward(side, qkv, ids, head_cols):
    sides, rows, _ = qkv.shape
    length = sides * rows
    count = length // tile_rows
    half = rows // tile_rows
    pairs = head_cols // 128

    def row_map(h, i, c):
        return ((i // half) ^ c[0], i % half, h)

    return pl.pallas_call(
        functools.partial(attend_forward_body, count, half),
        grid_spec=pltpu.PrefetchScalarGridSpec(
            num_scalar_prefetch=1,
            grid=(pairs, count),
            in_specs=[
                pl.BlockSpec((None, tile_rows, 128), row_map),
                pl.BlockSpec((sides, rows, 128), lambda h, i, c: (0, 0, pairs + h)),
                pl.BlockSpec((sides, rows, 128), lambda h, i, c: (0, 0, 2 * pairs + h)),
                pl.BlockSpec((1, length), lambda h, i, c: (0, 0)),
            ],
            out_specs=[
                pl.BlockSpec((None, tile_rows, 128), row_map),
                pl.BlockSpec((None, tile_rows, 2), lambda h, i, c: (h, i, 0)),
            ],
            scratch_shapes=[pltpu.VMEM((2, tile_rows, length), wide)],
        ),
        out_shape=[
            jax.ShapeDtypeStruct((sides, rows, head_cols), low),
            jax.ShapeDtypeStruct((pairs, length, 2), wide),
        ],
        name="attend_forward",
    )(side, qkv, qkv, qkv, ids)


def attend_backward_body(
    count, half, col_ref, q_ref, k_ref, v_ref, g_ref, ids_ref, lse_ref,
    gq_ref, gk_ref, gv_ref, p_ref, gp_ref, gk_acc, gv_acc,
):
    step = pl.program_id(1)
    side = col_ref[0]
    size = tile_rows
    lane = lax.broadcasted_iota(jnp.int32, (size, 128), 1)

    def key_tile(ref, j):
        return ref[(j // half) ^ side, (j % half) * size : (j % half + 1) * size, :]

    @pl.when(step == 0)
    def _():
        gk_acc[...] = jnp.zeros_like(gk_acc)
        gv_acc[...] = jnp.zeros_like(gv_acc)

    def variant(c):
        keys = min(c + 2, count)
        query = q_ref[...]
        grad = g_ref[...]
        query_turned = jnp.transpose(query.astype(wide)).astype(low)
        grad_turned = jnp.transpose(grad.astype(wide)).astype(low)
        ids_column = column_of(ids_ref[:, c * size : (c + 1) * size])
        out = None
        for head in range(2):
            mine = (lane < HEAD_DIM) if head == 0 else (lane >= HEAD_DIM)
            spot = slice(head * HEAD_DIM, (head + 1) * HEAD_DIM)
            part = jnp.where(mine, query, jnp.zeros_like(query)) * jnp.asarray(0.125, low)
            grad_part = jnp.where(mine, grad, jnp.zeros_like(grad))
            log_sum = lse_ref[:, head : head + 1]
            inner = None
            for j in range(keys):
                here = slice(j * size, (j + 1) * size)
                scores = dot_nt(part, key_tile(k_ref, j))
                grad_probs = dot_nt(grad_part, key_tile(v_ref, j))
                probs = jnp.exp(scores - log_sum)
                if j >= c:
                    mask = allowed_mask(ids_ref, ids_column, j * size, size)
                    probs = jnp.where(mask, probs, 0.0)
                p_ref[head, :, here] = probs
                gp_ref[head, :, here] = grad_probs
                piece = fold_lanes(probs * grad_probs, jnp.add)
                inner = piece if inner is None else inner + piece
                gv_acc[spot, here] += dot_nn(grad_turned[spot, :], probs.astype(low))
            inner = jnp.sum(inner, axis=1, keepdims=True)
            grad_query = None
            for j in range(keys):
                here = slice(j * size, (j + 1) * size)
                grad_scores = (p_ref[head, :, here] * (gp_ref[head, :, here] - inner)).astype(low)
                piece = dot_nn(grad_scores, key_tile(k_ref, j))
                grad_query = piece if grad_query is None else grad_query + piece
                gk_acc[spot, here] += dot_nn(query_turned[spot, :], grad_scores)
            out = grad_query if head == 0 else jnp.where(mine, grad_query, out)
        gq_ref[...] = (out * 0.125).astype(low)

    for c in range(count):
        pl.when(step == c)(functools.partial(variant, c))

    @pl.when(step == count - 1)
    def _():
        for j in range(count):
            here = slice(j * size, (j + 1) * size)
            rows = slice((j % half) * size, (j % half + 1) * size)
            gk_ref[(j // half) ^ side, rows, :] = jnp.transpose(gk_acc[:, here] * 0.125).astype(low)
            gv_ref[(j // half) ^ side, rows, :] = jnp.transpose(gv_acc[:, here]).astype(low)


def attend_backward(side, qkv, grad, ids, log_sums, head_cols):
    sides, rows, _ = qkv.shape
    length = sides * rows
    count = length // tile_rows
    half = rows // tile_rows
    pairs = head_cols // 128

    def row_map(h, i, c):
        return ((i // half) ^ c[0], i % half, h)

    row_spec = pl.BlockSpec((None, tile_rows, 128), row_map)
    whole = pl.BlockSpec((sides, rows, 128), lambda h, i, c: (0, 0, h))
    return pl.pallas_call(
        functools.partial(attend_backward_body, count, half),
        grid_spec=pltpu.PrefetchScalarGridSpec(
            num_scalar_prefetch=1,
            grid=(pairs, count),
            in_specs=[
                row_spec,
                pl.BlockSpec((sides, rows, 128), lambda h, i, c: (0, 0, pairs + h)),
                pl.BlockSpec((sides, rows, 128), lambda h, i, c: (0, 0, 2 * pairs + h)),
                row_spec,
                pl.BlockSpec((1, length), lambda h, i, c: (0, 0)),
                pl.BlockSpec((None, tile_rows, 2), lambda h, i, c: (h, i, 0)),
            ],
            out_specs=[row_spec, whole, whole],
            scratch_shapes=[
                pltpu.VMEM((2, tile_rows, length), wide),
                pltpu.VMEM((2, tile_rows, length), wide),
                pltpu.VMEM((128, length), wide),
                pltpu.VMEM((128, length), wide),
            ],
        ),
        out_shape=[jax.ShapeDtypeStruct((sides, rows, head_cols), low)] * 3,
        name="attend_backward",
    )(side, qkv, qkv, qkv, grad, ids, log_sums)


def layer_norm_parts(values, gain, bias):
    mean = jnp.mean(values, axis=-1, keepdims=True)
    centred = values - mean
    inverse = lax.rsqrt(jnp.mean(centred * centred, axis=-1, keepdims=True) + norm_eps)
    unit = centred * inverse
    return (unit * gain + bias, unit, inverse)


def norm_back(grad_normed, unit, inverse, gain):
    grad_unit = grad_normed * gain
    first_mean = jnp.mean(grad_unit, axis=-1, keepdims=True)
    second_mean = jnp.mean(grad_unit * unit, axis=-1, keepdims=True)
    return inverse * (grad_unit - first_mean - unit * second_mean)


def gelu_exact(values):
    return jax.nn.gelu(values, approximate=False)


def swap(values, axis, distance):
    size = lax.axis_size(axis)
    return lax.ppermute(values, axis, [(i, i ^ distance) for i in range(size)])


def gather_row(shard):
    size = lax.axis_size("row")
    if size != 4:
        return lax.all_gather(shard, "row", axis=0, tiled=True)
    me = lax.axis_index("row")
    rows = shard.shape[0]
    cut = rows // 2
    first, second = shard[:cut], shard[cut:]
    first_x, second_x = swap(first, "row", 1), swap(second, "row", 1)
    second_y, first_y = swap(second, "row", 2), swap(first, "row", 2)
    first_xy, second_xy = swap(first_x, "row", 2), swap(second_y, "row", 1)
    whole = jnp.zeros((size * rows, shard.shape[1]), shard.dtype)
    pieces = ((0, first, second), (1, first_x, second_x), (2, first_y, second_y), (3, first_xy, second_xy))
    for distance, upper, lower in pieces:
        base = (me ^ distance) * rows
        whole = lax.dynamic_update_slice(whole, upper, (base, 0))
        whole = lax.dynamic_update_slice(whole, lower, (base + cut, 0))
    return whole


def sum_line(values):
    size = lax.axis_size("dp")
    if size != 4:
        return lax.psum(values, "dp")
    me = lax.axis_index("dp")
    inner = (me == 1) | (me == 2)
    kept = values.astype(wide)
    kept = kept + lax.ppermute(values, "dp", [(0, 1), (3, 2)]).astype(wide)
    sent = kept.astype(values.dtype)
    total = (kept + lax.ppermute(sent, "dp", [(1, 2), (2, 1)]).astype(wide)).astype(values.dtype)
    outer = lax.ppermute(total, "dp", [(1, 0), (2, 3)])
    return jnp.where(inner, total, outer)


def reduce_weight(partial):
    width = partial.shape[1] // 2
    arrived = swap(partial[:, width:].astype(low), "col", 1)
    merged = partial[:, :width] + arrived.astype(wide)
    return reduce_rows(merged)


def reduce_rows(merged):
    size = lax.axis_size("row")
    if size != 4:
        share = lax.psum_scatter(merged.astype(low), "row", scatter_dimension=0, tiled=True)
        return sum_line(share).astype(wide)
    me = lax.axis_index("row")
    rows = merged.shape[0] // size
    cut = rows // 2

    def piece(distance, start, count):
        return lax.dynamic_slice_in_dim(merged, (me ^ distance) * rows + start, count, 0)

    from_y = swap(piece(3, 0, cut).astype(low), "row", 2)
    from_x = swap(piece(3, cut, cut).astype(low), "row", 1)
    to_x = piece(1, 0, rows) + jnp.pad(from_y.astype(wide), ((0, cut), (0, 0)))
    to_y = piece(2, 0, rows) + jnp.pad(from_x.astype(wide), ((cut, 0), (0, 0)))
    got_x = swap(to_x.astype(low), "row", 1)
    got_y = swap(to_y.astype(low), "row", 2)
    share = piece(0, 0, rows) + got_x.astype(wide) + got_y.astype(wide)
    return sum_line(share.astype(low)).astype(wide)


def sum_row_dp(values):
    if lax.axis_size("row") != 4:
        return lax.psum(values, ("dp", "row"))
    values = values + swap(values, "row", 1)
    values = values + swap(values, "row", 2)
    return sum_line(values)


def shards(
    tokens, timesteps, block_ids, table, gain_one, bias_one, w_query, w_key, w_value, b_query,
    b_value, w_out, b_out, gain_two, bias_two, w_up, b_up, w_down, b_down, cotangent,
):
    seq_count, local_len, model_width = tokens.shape
    assert seq_count == 1 and lax.axis_size("col") == 2
    head_cols = w_query.shape[1]
    hidden_cols = w_up.shape[1]
    col_index = lax.axis_index("col")
    row_index = lax.axis_index("row")
    row_size, dp_size = lax.axis_size("row"), lax.axis_size("dp")
    seq_index = lax.axis_index("dp") * row_size + row_index
    seq_total = dp_size * row_size
    side = jnp.reshape(col_index, (1,)).astype(jnp.int32)

    group_one = jnp.concatenate([w_query, w_key, w_value], axis=1).astype(low)
    group_two = jnp.concatenate([w_out.T, w_up], axis=1).astype(low)
    group_three = w_down.T.astype(low)
    in_proj = gather_row(group_one)
    out_up = gather_row(group_two)
    down_mine = gather_row(group_three)
    in_proj_other = swap(in_proj, "col", 1)
    out_up_other = swap(out_up, "col", 1)
    down_other = swap(down_mine, "col", 1)

    table_row = lax.dynamic_slice_in_dim(table, timesteps[0], 1, 0)
    start = tokens[0].astype(wide) + table_row
    normed_one, unit_one, inverse_one = layer_norm_parts(start, gain_one, bias_one)
    rows_mine = normed_one.astype(low)
    rows_both = jnp.stack([rows_mine, swap(rows_mine, "col", 1)])
    in_bias = jnp.concatenate([b_query, jnp.zeros_like(b_query), b_value])
    qkv = (
        jnp.einsum("ard,dh->arh", rows_both, in_proj, preferred_element_type=wide) + in_bias
    ).astype(low)
    mixed, log_sums = attend_forward(side, qkv, block_ids, head_cols)
    attended = jnp.concatenate([mixed[0], swap(mixed[1], "col", 1)], axis=1)

    out_turned = jnp.concatenate([out_up[:, :head_cols], out_up_other[:, :head_cols]], axis=1)
    up_full = jnp.concatenate([out_up[:, head_cols:], out_up_other[:, head_cols:]], axis=1)
    down_turned = jnp.concatenate([down_mine, down_other], axis=1)
    up_bias = jnp.concatenate([b_up, swap(b_up, "col", 1)])

    middle = start + (dot_nt(attended, out_turned) + b_out)
    normed_two, unit_two, inverse_two = layer_norm_parts(middle, gain_two, bias_two)
    rows_two = normed_two.astype(low)
    hidden_pre = dot_nn(rows_two, up_full) + up_bias
    hidden, gelu_back = jax.vjp(gelu_exact, hidden_pre)
    hidden = hidden.astype(low)
    layer_out = (middle + (dot_nt(hidden, down_turned) + b_down)).astype(low)

    cot = cotangent[0]
    grad_b_down = jnp.sum(cot, axis=0, dtype=wide)
    grad_pre = gelu_back(dot_nn(cot, down_turned))[0].astype(low)
    grad_b_up_wide = jnp.sum(grad_pre, axis=0, dtype=wide)
    own_down = reduce_weight(dot_tn(cot, hidden))
    own_up = reduce_weight(dot_tn(rows_two, grad_pre))
    grad_normed_two = dot_nt(grad_pre, up_full)
    grad_gain_two = jnp.sum(grad_normed_two * unit_two, axis=0)
    grad_bias_two = jnp.sum(grad_normed_two, axis=0)
    grad_middle = cot.astype(wide) + norm_back(grad_normed_two, unit_two, inverse_two, gain_two)
    grad_branch = grad_middle.astype(low)
    grad_b_out = jnp.sum(grad_branch, axis=0, dtype=wide)
    own_out = reduce_weight(dot_tn(grad_branch, attended))
    grad_attended = dot_nn(grad_branch, out_turned).astype(low)
    grad_heads = jnp.stack([grad_attended[:, :head_cols], swap(grad_attended[:, head_cols:], "col", 1)])

    grad_query, grad_key, grad_value = attend_backward(
        side, qkv, grad_heads, block_ids, log_sums, head_cols
    )
    grad_qkv = jnp.concatenate([grad_query, grad_key, grad_value], axis=2)
    own_in = reduce_rows(
        jnp.einsum("ard,arh->dh", rows_both, grad_qkv, preferred_element_type=wide)
    )
    grad_in_bias = jnp.sum(grad_qkv, axis=(0, 1), dtype=wide)
    grad_normed_one = dot_nt(grad_qkv[0], in_proj) + dot_nt(swap(grad_qkv[1], "col", 1), in_proj_other)
    grad_gain_one = jnp.sum(grad_normed_one * unit_one, axis=0)
    grad_bias_one = jnp.sum(grad_normed_one, axis=0)
    grad_tokens = grad_middle + norm_back(grad_normed_one, unit_one, inverse_one, gain_one)
    token_sum = jnp.sum(grad_tokens, axis=0)

    vectors = jnp.stack(
        [grad_gain_one, grad_bias_one, grad_b_out, grad_gain_two, grad_bias_two, grad_b_down, token_sum]
    )
    vectors = vectors + swap(vectors, "col", 1)
    grad_b_up = grad_b_up_wide[:hidden_cols] + swap(grad_b_up_wide[hidden_cols:], "col", 1)
    slot = lax.broadcasted_iota(jnp.int32, (seq_total, 1), 0) == seq_index
    sums_by_seq = jnp.where(slot, vectors[6:7], 0.0)
    steps_by_seq = jnp.where(slot, timesteps[0].astype(wide), 0.0)
    packed = jnp.concatenate(
        [
            vectors[:6].reshape(-1),
            grad_in_bias,
            grad_b_up,
            sums_by_seq.reshape(-1),
            steps_by_seq.reshape(-1),
        ]
    )
    pad = -packed.shape[0] % 1024
    packed = sum_row_dp(jnp.pad(packed, (0, pad)).reshape(-1, 128)).reshape(-1)
    place = 0
    taken = []
    for size in (6 * model_width, 3 * head_cols, hidden_cols, seq_total * model_width, seq_total):
        taken.append(packed[place : place + size])
        place += size
    six = taken[0].reshape(6, model_width)
    in_bias_sum = taken[1]
    step_onehot = (
        lax.broadcasted_iota(jnp.int32, (seq_total, table.shape[0]), 1)
        == taken[4][:, None].astype(jnp.int32)
    ).astype(wide)
    grad_table = jnp.einsum(
        "sv,sd->vd",
        step_onehot,
        taken[3].reshape(seq_total, model_width),
        precision=lax.Precision.HIGHEST,
        preferred_element_type=wide,
    )
    return (
        layer_out[None],
        grad_tokens[None],
        grad_table,
        six[0],
        six[1],
        own_in[:, :head_cols],
        own_in[:, head_cols : 2 * head_cols],
        own_in[:, 2 * head_cols :],
        in_bias_sum[:head_cols],
        in_bias_sum[2 * head_cols :],
        own_out.T,
        six[2],
        six[3],
        six[4],
        own_up,
        taken[2],
        own_down.T,
        six[5],
    )


def solution(mesh):
    return jax.shard_map(
        shards,
        mesh=mesh,
        in_specs=(
            P(("dp", "row"), "col", None),
            P(("dp", "row")),
            P(("dp", "row"), None),
            P(),
            P(),
            P(),
            P("row", "col"),
            P("row", "col"),
            P("row", "col"),
            P("col"),
            P("col"),
            P("col", "row"),
            P(),
            P(),
            P(),
            P("row", "col"),
            P("col"),
            P("col", "row"),
            P(),
            P(("dp", "row"), "col", None),
        ),
        out_specs=(
            P(("dp", "row"), "col", None),
            P(("dp", "row"), "col", None),
            P(),
            P(),
            P(),
            P("row", "col"),
            P("row", "col"),
            P("row", "col"),
            P("col"),
            P("col"),
            P("col", "row"),
            P(),
            P(),
            P(),
            P("row", "col"),
            P("col"),
            P("col", "row"),
            P(),
        ),
        check_vma=False,
    )
```

time: 1390 us -> 529 us (0.38)
  waiting for transfers between devices: 567 us -> 100 us
  matrix products: 470 us -> 116 us
  other arithmetic: 177 us -> 44.9 us
  Pallas kernels: 0 us -> 117 us
  blocking collectives: 91.2 us -> 0 us
  starting transfers between devices: 0.51 us -> 88.4 us
  between operations: 17.5 us -> 2.95 us
    psum x2 -> x0, waiting for transfers between devices: 473 us -> none  [the longest x1 342 us: shards(): lax.psum((grad_w_query, grad_w_key, grad_w_value, grad_up, grad_out_proj,...]
    dot_general x47 -> x14, matrix products: 470 us -> 116 us  [the longest x3 56.1 us: dot_nn(): lax.dot_general(left, right, (((1,), (0,)), ((), ())), preferred_element_...]
    pallas_call x0 -> x2, Pallas kernels: none -> 117 us  [the longest x1 74.7 us: attend_backward(): pl.pallas_call(functools.partial(attend_backward_body, count, half), grid...]
    ppermute x0 -> x64, waiting for transfers between devices: none -> 100 us  [the longest x49 55.6 us: swap(): return lax.ppermute(values, axis, [(i, i ^ distance) for i in range(size)])]
    ppermute x0 -> x64, starting transfers between devices: none -> 88.4 us  [the longest x49 42.8 us: swap(): return lax.ppermute(values, axis, [(i, i ^ distance) for i in range(size)])]
    convert_element_type x13 -> x22, other arithmetic: 92.6 us -> 17.9 us  [the longest x6 5.55 us: reduce_rows(): return sum_line(share.astype(low)).astype(wide)]
    all_gather x6 -> x0, waiting for transfers between devices: 66.7 us -> none  [the longest x1 21 us: shards(): lax.all_gather(down_low, 'row', axis=1, tiled=True)]
    reduce_sum x10 -> x3, other arithmetic: 69.4 us -> 5.06 us  [the longest x1 2.58 us: shards(): token_sum = jnp.sum(grad_tokens, axis=0)]
  transfers between devices with their start and end apart: 12 -> 64, of which waited for: 9 -> 18; matrix products, arithmetic and copies ran while one was open for 8% -> 39% of each run, Pallas kernels for 0% -> 22%
where the time goes in v1:
time: 529 us; the launch traced here: 522 us
  Pallas kernels  117 us (22%)
  matrix products  116 us (22%)
  waiting for transfers between devices  100 us (19%)
  starting transfers between devices  88.4 us (17%)
  local copies, waits for them, and re-layouts  52.9 us (10%)
  other arithmetic  44.9 us (8%)
    pallas_call x1, Pallas kernels, attend_backward(): pl.pallas_call(functools.partial(attend_backward_body, count, half), grid...  74.7 us
    dot_general x3, matrix products, dot_nn(): lax.dot_general(left, right, (((1,), (0,)), ((), ())), preferred_element_...  56.1 us
    ppermute x49, waiting for transfers between devices, swap(): return lax.ppermute(values, axis, [(i, i ^ distance) for i in range(size)])  55.6 us
    ppermute x49, starting transfers between devices, swap(): return lax.ppermute(values, axis, [(i, i ^ distance) for i in range(size)])  42.8 us
    pallas_call x1, Pallas kernels, attend_forward(): pl.pallas_call(functools.partial(attend_forward_body, count, half), grid_...  41.9 us
    ppermute x5, starting transfers between devices, sum_line(): kept = kept + lax.ppermute(values, 'dp', [(0, 1), (3, 2)]).astype(wide)  35.6 us
    dot_general x5, matrix products, dot_nt(): lax.dot_general(left, right, (((1,), (1,)), ((), ())), preferred_element_...  29.6 us
    ppermute x5, waiting for transfers between devices, sum_line(): outer = lax.ppermute(total, 'dp', [(1, 0), (2, 3)])  24 us
  transfers between devices with their start and end apart: 64, of which 18 were waited for; matrix products, arithmetic and copies ran while one was open for 39% of the time, Pallas kernels for 22%

profile of v1, /device:TPU:0, one launch (start us, length us, event | category | flops | bytes accessed | tf_op | source)
XLA Modules:
  0.0 522.1 jit_solution(11106779204413878030)
XLA Ops:
  0.7 2.3 convert.48
  6.7 2.9 collective-permute-start.8
  11.2 1.9 constant_dynamic-update-slice_fusion.14
  20.1 1.9 fusion.16
  22.0 2.1 fusion.30
  24.2 1.9 fusion.24
  35.0 5.9 %collective-permute-done.2 = bf16[96,1152]{1,0:T(8,128)(2,1)S(1)} collective-permute-done((bf16[96,1152]{1,0:T(8,128)(2,1)S(1)}, bf16[96,1152]{1,0:T(8,128)(2,1)S(1)}, u32[]{:S(2)}, u32[]{:S(2)}) %collective-permute-start.2) | collective-permute-done | bytes 221216 | tf_op jit(solution)/shard_map/ppermute | solution.py:259
  43.1 5.5 %collective-permute-done.3 = bf16[96,1152]{1,0:T(8,128)(2,1)S(1)} collective-permute-done((bf16[96,1152]{1,0:T(8,128)(2,1)}, bf16[96,1152]{1,0:T(8,128)(2,1)S(1)}, u32[]{:S(2)}, u32[]{:S(2)}) %collective-permute-start.3) | collective-permute-done | bytes 221216 | tf_op jit(solution)/shard_map/ppermute | solution.py:259
  50.0 5.2 %collective-permute-done.4 = bf16[96,1152]{1,0:T(8,128)(2,1)S(1)} collective-permute-done((bf16[96,1152]{1,0:T(8,128)(2,1)S(1)}, bf16[96,1152]{1,0:T(8,128)(2,1)S(1)}, u32[]{:S(2)}, u32[]{:S(2)}) %collective-permute-start.4) | collective-permute-done | bytes 221216 | tf_op jit(solution)/shard_map/ppermute | solution.py:259
  66.1 6.1 %collective-permute-done.12 = bf16[96,1920]{1,0:T(8,128)(2,1)S(1)} collective-permute-done((bf16[96,1920]{1,0:T(8,128)(2,1)}, bf16[96,1920]{1,0:T(8,128)(2,1)S(1)}, u32[]{:S(2)}, u32[]{:S(2)}) %collective-permute-start.12) | collective-permute-done | bytes 368672 | tf_op jit(solution)/shard_map/ppermute | solution.py:259
  77.1 3.9 collective-permute-done.17
  83.0 4.5 collective-permute-done.5
  90.5 3.3 collective-permute-done.6
  95.5 7.9 %add_convert_fusion.q_ref.k_ref.v_ref = bf16[2,1024,1152]{2,1,0:T(8,128)(2,1)} fusion(f32[1152]{0:T(1024)S(1)} %pad_maximum_fusion.21, bf16[1,1024,768]{2,1,0:T(8,128)(2,1)S(1)} %bitcast.150, bf16[1,1024,768]{2,1,0:T(8,128)(2,1)S(1)} %fusion.35, bf16[768,1152]{1,0:T(8,128)(2,1)} %constant_dynamic-update-slice_fusion.16), kind=kOutput, calls=%fused_computation.27 | convolution fusion | flops 3630170112 | bytes 9638400 | tf_op jit(solution)/shard_map/ard,dh->arh/dot_general | solution.py:365
  103.4 41.9 %attend_forward.1 = (bf16[2,1024,384]{2,1,0:T(8,128)(2,1)}, f32[3,2048,2]{2,1,0:T(8,128)}) custom-call(s32[1]{0:T(128)} %bitcast.2.col_ref, bf16[2,1024,1152]{2,1,0:T(8,128)(2,1)} %add_convert_fusion.q_ref.k_ref.v_ref, bf16[2,1024,1152]{2,1,0:T(8,128)(2,1)} %add_convert_fusion.q_ref.k_ref.v_ref, bf16[2,1024,1152]{2,1,0:T(8,128)(2,1)} %add_convert_fusion.q_ref.k_ref.v_ref, ...), custom_call_target="tpu_custom_call" | custom-call | tf_op jit(solution)/shard_map/attend_forward/pallas_call | solution.py:107
  146.9 1.9 constant_dynamic-update-slice_fusion.3
  152.7 1.9 slice.200
  158.5 2.4 slice.201
  161.0 37.9 %multiply_convert_fusion = (bf16[1024,3072]{1,0:T(8,128)(2,1)}, f32[1024,3072]{1,0:T(8,128)}, f32[1024,3072]{1,0:T(8,128)}) fusion(f32[3072]{0:T(1024)S(1)} %pad_maximum_fusion.20, bf16[768,1536]{1,0:T(8,128)(2,1)S(1)} %slice.201, bf16[768,1536]{1,0:T(8,128)(2,1)S(1)} %slice.200, f32[1024,768]{1,0:T(8,128)S(1)} %get-tuple-element.85, ...), kind=kOutput, calls=%fused_computation.12 | convolution fusion | flops 5052825600 | bytes 39348224 | tf_op jit(solution)/shard_map/dot_general | solution.py:19
  200.3 16.8 %convert_reduce_fusion = (f32[3072]{0:T(1024)S(1)}, bf16[1024,3072]{1,0:T(8,128)(2,1)}) fusion(f32[1024,3072]{1,0:T(8,128)} %get-tuple-element.41, bf16[768,1536]{1,0:T(8,128)(2,1)} %copy-done.51, bf16[768,1536]{1,0:T(8,128)(2,1)} %constant_dynamic-update-slice_fusion, bf16[1,1024,768]{2,1,0:T(8,128)(2,1)S(1)} %copy-done.26, ...), kind=kOutput, calls=%fused_computation.11 | convolution fusion | flops 4894749696 | bytes 37773312 | tf_op jit(solution)/shard_map/dot_general | solution.py:19
  217.1 10.3 %multiply_reduce_fusion = (f32[768]{0:T(1024)S(1)}, f32[1024]{0:T(1024)S(1)}, f32[1024]{0:T(1024)S(1)}, f32[768]{0:T(1024)S(1)}, f32[1024,768]{1,0:T(8,128)S(1)}) fusion(f32[1024,768]{1,0:T(8,128)} %copy-done.5, f32[1024]{0:T(1024)S(1)} %add_rsqrt_fusion, f32[1024]{0:T(1024)S(1)} %broadcast_multiply_fusion.4, f32[768]{0:T(1024)S(1)} %copy-done.40, ...), kind=kOutput, calls=%fused_computation.64 | convolution fusion | flops 4848349184 | bytes 17327104 | tf_op jit(solution)/shard_map/dot_general | solution.py:23
  227.5 5.7 %fusion.67 = f32[768,3072]{1,0:T(8,128)S(1)} fusion(bf16[1024,3072]{1,0:T(8,128)(2,1)S(1)} %copy-done.13, f32[1024,768]{1,0:T(8,128)S(1)} %copy-done.6, f32[768]{0:T(1024)S(1)} %copy-done.43, f32[768]{0:T(1024)S(1)} %copy-done.40, f32[1024]{0:T(1024)S(1)} %add_rsqrt_fusion, f32[1024]{0:T(1024)S(1)} %broadcast_multiply_fusion.4), kind=kOutput, calls=%fused_computation.212 | convolution fusion | flops 4835770368 | bytes 18888704 | tf_op jit(solution)/shard_map/dot_general | solution.py:27
  244.1 7.5 %convolution_bitcast_fusion = f32[768,3072]{1,0:T(8,128)} fusion(bf16[1024,3072]{1,0:T(8,128)(2,1)S(1)} %bitcast.153, bf16[1,1024,768]{2,1,0:T(8,128)(2,1)S(1)} %copy-done.26), kind=kOutput, calls=%fused_computation.28 | convolution fusion | flops 4831838208 | bytes 17301504 | tf_op jit(solution)/shard_map/dot_general | solution.py:27
  254.8 74.7 %attend_backward.1 = (bf16[2,1024,384]{2,1,0:T(8,128)(2,1)}, bf16[2,1024,384]{2,1,0:T(8,128)(2,1)}, bf16[2,1024,384]{2,1,0:T(8,128)(2,1)}) custom-call(s32[1]{0:T(128)} %bitcast.2.col_ref, bf16[2,1024,1152]{2,1,0:T(8,128)(2,1)} %add_convert_fusion.q_ref.k_ref.v_ref, bf16[2,1024,1152]{2,1,0:T(8,128)(2,1)} %add_convert_fusion.q_ref.k_ref.v_ref, ...), custom_call_target="tpu_custom_call" | custom-call | tf_op jit(solution)/shard_map/attend_backward/pallas_call | solution.py:212
  333.4 4.4 convolution_bitcast_fusion.1
  340.4 3.3 collective-permute-start.45
  348.1 9.2 %fusion.42 = bf16[1,1024,768]{2,1,0:T(8,128)(2,1)} fusion(f32[1024,768]{1,0:T(8,128)S(1)} %copy-done.7, f32[768]{0:T(1024)S(1)} %copy-done.58, bf16[1024,3072]{1,0:T(8,128)(2,1)} %get-tuple-element.40, bf16[768,1536]{1,0:T(8,128)(2,1)S(1)} %copy-done.52, bf16[768,1536]{1,0:T(8,128)(2,1)} %constant_dynamic-update-slice_fusion), kind=kOutput, calls=%fused_computation.82 | convolution fusion | flops 4843634688 | bytes 15731712 | tf_op jit(solution)/shard_map/dot_general | solution.py:23
  358.0 2.6 slice.270
  361.6 5.9 %collective-permute-start.37 = (bf16[192,1152]{1,0:T(8,128)(2,1)S(1)}, bf16[192,1152]{1,0:T(8,128)(2,1)S(1)}, u32[]{:S(2)}, u32[]{:S(2)}) collective-permute-start(bf16[192,1152]{1,0:T(8,128)(2,1)S(1)} %add_convert_fusion.12), channel_id=1, source_target_pairs={{0,8},{24,16},{1,9},{25,17},{2,10},{26,18},{3,11},{27,19},{4,12},{... | collective-permute-start | bytes 1327112 | tf_op jit(solution)/shard_map/ppermute | solution.py:289
  369.1 8.2 %collective-permute-done.37 = bf16[192,1152]{1,0:T(8,128)(2,1)S(1)} collective-permute-done((bf16[192,1152]{1,0:T(8,128)(2,1)S(1)}, bf16[192,1152]{1,0:T(8,128)(2,1)S(1)}, u32[]{:S(2)}, u32[]{:S(2)}) %collective-permute-start.37) | collective-permute-done | bytes 442400 | tf_op jit(solution)/shard_map/ppermute | solution.py:289
  381.8 2.3 slice_add_fusion.1
  387.9 3.0 slice_add_fusion
  393.8 3.7 fusion.76
  397.6 4.7 fusion.29
  402.3 2.6 fusion.68
  411.6 2.9 collective-permute-done.59
  414.6 1.8 add_convert_fusion.6
  416.4 2.0 collective-permute-start.60
  418.4 9.4 %collective-permute-done.28 = f32[160,128]{1,0:T(8,128)S(1)} collective-permute-done((f32[160,128]{1,0:T(8,128)S(1)}, f32[160,128]{1,0:T(8,128)S(1)}, u32[]{:S(2)}, u32[]{:S(2)}) %collective-permute-start.28) | collective-permute-done | bytes 81952 | tf_op jit(solution)/shard_map/ppermute | solution.py:259
  431.2 6.8 %collective-permute-done.29 = f32[160,128]{1,0:T(8,128)S(1)} collective-permute-done((f32[160,128]{1,0:T(8,128)S(1)}, f32[160,128]{1,0:T(8,128)S(1)}, u32[]{:S(2)}, u32[]{:S(2)}) %collective-permute-start.29) | collective-permute-done | bytes 81952 | tf_op jit(solution)/shard_map/ppermute | solution.py:259
  438.0 15.8 %collective-permute-start.30 = (f32[160,128]{1,0:T(8,128)S(1)}, f32[160,128]{1,0:T(8,128)S(1)}, u32[]{:S(2)}, u32[]{:S(2)}) collective-permute-start(f32[160,128]{1,0:T(8,128)S(1)} %fusion.86), channel_id=1, source_target_pairs={{0,8},{24,16},{1,9},{25,17},{2,10},{26,18},{3,11},{27,19},{4,12},{... | collective-permute-start | bytes 245768 | tf_op jit(solution)/shard_map/ppermute | solution.py:289
  458.2 6.0 %collective-permute-start.53 = (bf16[192,1536]{1,0:T(8,128)(2,1)S(1)}, bf16[192,1536]{1,0:T(8,128)(2,1)S(1)}, u32[]{:S(2)}, u32[]{:S(2)}) collective-permute-start(bf16[192,1536]{1,0:T(8,128)(2,1)S(1)} %add_convert_fusion.8), channel_id=1, source_target_pairs={{0,8},{24,16},{1,9},{25,17},{2,10},{26,18},{3,11},{27,19},{4,12},{... | collective-permute-start | bytes 1769480 | tf_op jit(solution)/shard_map/ppermute | solution.py:289
  467.1 4.6 collective-permute-start.61
  471.8 3.1 fusion.51
  475.5 2.5 collective-permute-done.53
  478.8 9.0 %collective-permute-done.61 = bf16[192,1536]{1,0:T(8,128)(2,1)S(1)} collective-permute-done((bf16[192,1536]{1,0:T(8,128)(2,1)S(1)}, bf16[192,1536]{1,0:T(8,128)(2,1)S(1)}, u32[]{:S(2)}, u32[]{:S(2)}) %collective-permute-start.61) | collective-permute-done | bytes 589856 | tf_op jit(solution)/shard_map/ppermute | solution.py:289
  495.7 15.4 %collective-permute-done.55 = bf16[192,1536]{1,0:T(8,128)(2,1)S(1)} collective-permute-done((bf16[192,1536]{1,0:T(8,128)(2,1)S(1)}, bf16[192,1536]{1,0:T(8,128)(2,1)S(1)}, u32[]{:S(2)}, u32[]{:S(2)}) %collective-permute-start.55) | collective-permute-done | bytes 589856 | tf_op jit(solution)/shard_map/ppermute | solution.py:292
  512.2 8.6 %collective-permute-done.63 = bf16[192,1536]{1,0:T(8,128)(2,1)S(1)} collective-permute-done((bf16[192,1536]{1,0:T(8,128)(2,1)S(1)}, bf16[192,1536]{1,0:T(8,128)(2,1)S(1)}, u32[]{:S(2)}, u32[]{:S(2)}) %collective-permute-start.63) | collective-permute-done | bytes 589856 | tf_op jit(solution)/shard_map/ppermute | solution.py:292
  (354 shorter events, 124.8 us)
Async XLA Ops:
  6.7 50.1 %collective-permute-start.8 = (bf16[96,1920]{1,0:T(8,128)(2,1)}, bf16[96,1920]{1,0:T(8,128)(2,1)}, u32[]{:S(2)}, u32[]{:S(2)}) collective-permute-start(bf16[96,1920]{1,0:T(8,128)(2,1)} %get-tuple-element.45), channel_id=1, source_target_pairs={{0,2},{2,0},{4,6},{6,4},{1,3},{3,1},{5,7},{7,5},{8,10},{10,8},{12,... | collective-permute-start | bytes 1105928 | tf_op jit(solution)/shard_map/ppermute | solution.py:259
  9.7 50.9 %collective-permute-start.10 = (bf16[96,1920]{1,0:T(8,128)(2,1)}, bf16[96,1920]{1,0:T(8,128)(2,1)}, u32[]{:S(2)}, u32[]{:S(2)}) collective-permute-start(bf16[96,1920]{1,0:T(8,128)(2,1)} %get-tuple-element.45), channel_id=1, source_target_pairs={{0,4},{2,6},{4,0},{6,2},{1,5},{3,7},{5,1},{7,3},{8,12},{10,14},{12... | collective-permute-start | bytes 1105928 | tf_op jit(solution)/shard_map/ppermute | solution.py:259
  13.1 45.7 %collective-permute-start.9 = (bf16[96,1920]{1,0:T(8,128)(2,1)}, bf16[96,1920]{1,0:T(8,128)(2,1)}, u32[]{:S(2)}, u32[]{:S(2)}) collective-permute-start(bf16[96,1920]{1,0:T(8,128)(2,1)} %get-tuple-element.43), channel_id=1, source_target_pairs={{0,2},{2,0},{4,6},{6,4},{1,3},{3,1},{5,7},{7,5},{8,10},{10,8},{12,... | collective-permute-start | bytes 1105928 | tf_op jit(solution)/shard_map/ppermute | solution.py:259
  17.9 15.3 %collective-permute-start.1 = (bf16[96,1152]{1,0:T(8,128)(2,1)}, bf16[96,1152]{1,0:T(8,128)(2,1)}, u32[]{:S(2)}, u32[]{:S(2)}) collective-permute-start(bf16[96,1152]{1,0:T(8,128)(2,1)} %get-tuple-element.75), channel_id=1, source_target_pairs={{0,2},{2,0},{4,6},{6,4},{1,3},{3,1},{5,7},{7,5},{8,10},{10,8},{12,... | collective-permute-start | bytes 663560 | tf_op jit(solution)/shard_map/ppermute | solution.py:259
  19.4 13.3 %collective-permute-start.15 = (f32[1536]{0:T(1024)S(1)}, f32[1536]{0:T(1024)S(1)}, u32[]{:S(2)}, u32[]{:S(2)}) collective-permute-start(f32[1536]{0:T(1024)S(1)} %copy-done.47), channel_id=1, source_target_pairs={{0,1},{1,0},{2,3},{3,2},{4,5},{5,4},{6,7},{7,6},{8,9},{9,8},{10,11... | collective-permute-start | bytes 18440 | tf_op jit(solution)/shard_map/ppermute | solution.py:259
  32.7 29.7 %collective-permute-start.11 = (bf16[96,1920]{1,0:T(8,128)(2,1)}, bf16[96,1920]{1,0:T(8,128)(2,1)S(1)}, u32[]{:S(2)}, u32[]{:S(2)}) collective-permute-start(bf16[96,1920]{1,0:T(8,128)(2,1)} %get-tuple-element.43), channel_id=1, source_target_pairs={{0,4},{2,6},{4,0},{6,2},{1,5},{3,7},{5,1},{7,3},{8,12},{10,14},{12... | collective-permute-start | bytes 1105928 | tf_op jit(solution)/shard_map/ppermute | solution.py:259
  55.3 21.0 %collective-permute-start.16 = (bf16[96,1536]{1,0:T(8,128)(2,1)}, bf16[96,1536]{1,0:T(8,128)(2,1)S(1)}, u32[]{:S(2)}, u32[]{:S(2)}) collective-permute-start(bf16[96,1536]{1,0:T(8,128)(2,1)} %get-tuple-element.72), channel_id=1, source_target_pairs={{0,2},{2,0},{4,6},{6,4},{1,3},{3,1},{5,7},{7,5},{8,10},{10,8},{12,... | collective-permute-start | bytes 884744 | tf_op jit(solution)/shard_map/ppermute | solution.py:259
  56.8 90.1 %collective-permute-start.18 = (bf16[96,1536]{1,0:T(8,128)(2,1)}, bf16[96,1536]{1,0:T(8,128)(2,1)}, u32[]{:S(2)}, u32[]{:S(2)}) collective-permute-start(bf16[96,1536]{1,0:T(8,128)(2,1)} %get-tuple-element.72), channel_id=1, source_target_pairs={{0,4},{2,6},{4,0},{6,2},{1,5},{3,7},{5,1},{7,3},{8,12},{10,14},{12... | collective-permute-start | bytes 884744 | tf_op jit(solution)/shard_map/ppermute | solution.py:259
  58.8 36.6 %collective-permute-start = (bf16[1024,768]{1,0:T(8,128)(2,1)}, bf16[1024,768]{1,0:T(8,128)(2,1)S(1)}, u32[]{:S(2)}, u32[]{:S(2)}) collective-permute-start(bf16[1024,768]{1,0:T(8,128)(2,1)} %fusion.24), channel_id=1, source_target_pairs={{0,1},{1,0},{2,3},{3,2},{4,5},{5,4},{6,7},{7,6},{8,9},{9,8},{10,11... | collective-permute-start | bytes 4718600 | tf_op jit(solution)/shard_map/ppermute | solution.py:259
  60.6 11.6 %collective-permute-start.12 = (bf16[96,1920]{1,0:T(8,128)(2,1)}, bf16[96,1920]{1,0:T(8,128)(2,1)S(1)}, u32[]{:S(2)}, u32[]{:S(2)}) collective-permute-start(bf16[96,1920]{1,0:T(8,128)(2,1)} %collective-permute-done.8), channel_id=1, source_target_pairs={{0,4},{2,6},{4,0},{6,2},{1,5},{3,7},{5,1},{7,3},{8,12},{10,14},{12... | collective-permute-start | bytes 1105928 | tf_op jit(solution)/shard_map/ppermute | solution.py:259
  62.4 11.6 %collective-permute-start.13 = (bf16[96,1920]{1,0:T(8,128)(2,1)S(1)}, bf16[96,1920]{1,0:T(8,128)(2,1)S(1)}, u32[]{:S(2)}, u32[]{:S(2)}) collective-permute-start(bf16[96,1920]{1,0:T(8,128)(2,1)S(1)} %collective-permute-done.11), channel_id=1, source_target_pairs={{0,2},{2,0},{4,6},{6,4},{1,3},{3,1},{5,7},{7,5},{8,10},{10,8},{12,... | collective-permute-start | bytes 1105928 | tf_op jit(solution)/shard_map/ppermute | solution.py:259
  73.9 15.2 %collective-permute-start.19 = (bf16[96,1536]{1,0:T(8,128)(2,1)S(1)}, bf16[96,1536]{1,0:T(8,128)(2,1)S(1)}, u32[]{:S(2)}, u32[]{:S(2)}) collective-permute-start(bf16[96,1536]{1,0:T(8,128)(2,1)S(1)} %copy-done.34), channel_id=1, source_target_pairs={{0,4},{2,6},{4,0},{6,2},{1,5},{3,7},{5,1},{7,3},{8,12},{10,14},{12... | collective-permute-start | bytes 884744 | tf_op jit(solution)/shard_map/ppermute | solution.py:259
  76.3 78.3 %collective-permute-start.14 = (bf16[768,1920]{1,0:T(8,128)(2,1)}, bf16[768,1920]{1,0:T(8,128)(2,1)}, u32[]{:S(2)}, u32[]{:S(2)}) collective-permute-start(bf16[768,1920]{1,0:T(8,128)(2,1)} %constant_dynamic-update-slice_fusion.8), channel_id=1, source_target_pairs={{0,1},{1,0},{2,3},{3,2},{4,5},{5,4},{6,7},{7,6},{8,9},{9,8},{10,11... | collective-permute-start | bytes 8847368 | tf_op jit(solution)/shard_map/ppermute | solution.py:259
  89.1 60.7 %collective-permute-start.20 = (bf16[96,1536]{1,0:T(8,128)(2,1)S(1)}, bf16[96,1536]{1,0:T(8,128)(2,1)S(1)}, u32[]{:S(2)}, u32[]{:S(2)}) collective-permute-start(bf16[96,1536]{1,0:T(8,128)(2,1)S(1)} %collective-permute-done.16), channel_id=1, source_target_pairs={{0,4},{2,6},{4,0},{6,2},{1,5},{3,7},{5,1},{7,3},{8,12},{10,14},{12... | collective-permute-start | bytes 884744 | tf_op jit(solution)/shard_map/ppermute | solution.py:259
  93.8 56.8 %collective-permute-start.21 = (bf16[96,1536]{1,0:T(8,128)(2,1)S(1)}, bf16[96,1536]{1,0:T(8,128)(2,1)S(1)}, u32[]{:S(2)}, u32[]{:S(2)}) collective-permute-start(bf16[96,1536]{1,0:T(8,128)(2,1)S(1)} %collective-permute-done.19), channel_id=1, source_target_pairs={{0,2},{2,0},{4,6},{6,4},{1,3},{3,1},{5,7},{7,5},{8,10},{10,8},{12,... | collective-permute-start | bytes 884744 | tf_op jit(solution)/shard_map/ppermute | solution.py:259
  146.8 9.4 %collective-permute-start.7 = (bf16[1024,384]{1,0:T(8,128)(2,1)S(1)}, bf16[1024,384]{1,0:T(8,128)(2,1)S(1)}, u32[]{:S(2)}, u32[]{:S(2)}) collective-permute-start(bf16[1024,384]{1,0:T(8,128)(2,1)S(1)} %get-tuple-element.62), channel_id=1, source_target_pairs={{0,1},{1,0},{2,3},{3,2},{4,5},{5,4},{6,7},{7,6},{8,9},{9,8},{10,11... | collective-permute-start | bytes 2359304 | tf_op jit(solution)/shard_map/ppermute | solution.py:259
  149.5 242.3 %collective-permute-start.25 = (bf16[768,1152]{1,0:T(8,128)(2,1)}, bf16[768,1152]{1,0:T(8,128)(2,1)}, u32[]{:S(2)}, u32[]{:S(2)}) collective-permute-start(bf16[768,1152]{1,0:T(8,128)(2,1)} %constant_dynamic-update-slice_fusion.16), channel_id=1, source_target_pairs={{0,1},{1,0},{2,3},{3,2},{4,5},{5,4},{6,7},{7,6},{8,9},{9,8},{10,11... | collective-permute-start | bytes 5308424 | tf_op jit(solution)/shard_map/ppermute | solution.py:259
  151.3 47.5 %collective-permute-start.22 = (bf16[768,1536]{1,0:T(8,128)(2,1)}, bf16[768,1536]{1,0:T(8,128)(2,1)S(1)}, u32[]{:S(2)}, u32[]{:S(2)}) collective-permute-start(bf16[768,1536]{1,0:T(8,128)(2,1)} %constant_dynamic-update-slice_fusion), channel_id=1, source_target_pairs={{0,1},{1,0},{2,3},{3,2},{4,5},{5,4},{6,7},{7,6},{8,9},{9,8},{10,11... | collective-permute-start | bytes 7077896 | tf_op jit(solution)/shard_map/ppermute | solution.py:259
  239.2 14.2 %collective-permute-start.23 = (bf16[1024,384]{1,0:T(8,128)(2,1)S(1)}, bf16[1024,384]{1,0:T(8,128)(2,1)S(1)}, u32[]{:S(2)}, u32[]{:S(2)}) collective-permute-start(bf16[1024,384]{1,0:T(8,128)(2,1)S(1)} %get-tuple-element.60), channel_id=1, source_target_pairs={{0,1},{1,0},{2,3},{3,2},{4,5},{5,4},{6,7},{7,6},{8,9},{9,8},{10,11... | collective-permute-start | bytes 2359304 | tf_op jit(solution)/shard_map/ppermute | solution.py:259
  241.2 139.1 %collective-permute-start.48 = (bf16[768,1536]{1,0:T(8,128)(2,1)}, bf16[768,1536]{1,0:T(8,128)(2,1)}, u32[]{:S(2)}, u32[]{:S(2)}) collective-permute-start(bf16[768,1536]{1,0:T(8,128)(2,1)} %slice.271), channel_id=1, source_target_pairs={{0,1},{1,0},{2,3},{3,2},{4,5},{5,4},{6,7},{7,6},{8,9},{9,8},{10,11... | collective-permute-start | bytes 7077896 | tf_op jit(solution)/shard_map/ppermute | solution.py:259
  241.7 9.9 %collective-permute-start.41 = (bf16[96,384]{1,0:T(8,128)(2,1)S(1)}, bf16[96,384]{1,0:T(8,128)(2,1)S(1)}, u32[]{:S(2)}, u32[]{:S(2)}) collective-permute-start(bf16[96,384]{1,0:T(8,128)(2,1)S(1)} %get-tuple-element.65), channel_id=1, source_target_pairs={{0,4},{2,6},{4,0},{6,2},{1,5},{3,7},{5,1},{7,3},{8,12},{10,14},{12... | collective-permute-start | bytes 221192 | tf_op jit(solution)/shard_map/ppermute | solution.py:259
  251.7 87.8 %collective-permute-start.44 = (bf16[192,384]{1,0:T(8,128)(2,1)S(1)}, bf16[192,384]{1,0:T(8,128)(2,1)S(1)}, u32[]{:S(2)}, u32[]{:S(2)}) collective-permute-start(bf16[192,384]{1,0:T(8,128)(2,1)S(1)} %get-tuple-element.64), channel_id=1, source_target_pairs={{0,4},{2,6},{4,0},{6,2},{1,5},{3,7},{5,1},{7,3},{8,12},{10,14},{12... | collective-permute-start | bytes 442376 | tf_op jit(solution)/shard_map/ppermute | solution.py:259
  252.5 87.8 %collective-permute-start.42 = (bf16[192,384]{1,0:T(8,128)(2,1)S(1)}, bf16[192,384]{1,0:T(8,128)(2,1)S(1)}, u32[]{:S(2)}, u32[]{:S(2)}) collective-permute-start(bf16[192,384]{1,0:T(8,128)(2,1)S(1)} %get-tuple-element.63), channel_id=1, source_target_pairs={{0,2},{2,0},{4,6},{6,4},{1,3},{3,1},{5,7},{7,5},{8,10},{10,8},{12,... | collective-permute-start | bytes 442376 | tf_op jit(solution)/shard_map/ppermute | solution.py:259
  340.4 20.2 %collective-permute-start.45 = (bf16[192,384]{1,0:T(8,128)(2,1)S(1)}, bf16[192,384]{1,0:T(8,128)(2,1)S(1)}, u32[]{:S(2)}, u32[]{:S(2)}) collective-permute-start(bf16[192,384]{1,0:T(8,128)(2,1)S(1)} %add_convert_fusion.16), channel_id=1, source_target_pairs={{0,8},{24,16},{1,9},{25,17},{2,10},{26,18},{3,11},{27,19},{4,12},{... | collective-permute-start | bytes 442376 | tf_op jit(solution)/shard_map/ppermute | solution.py:289
  346.5 14.2 %collective-permute-start.36 = (bf16[192,1152]{1,0:T(8,128)(2,1)}, bf16[192,1152]{1,0:T(8,128)(2,1)S(1)}, u32[]{:S(2)}, u32[]{:S(2)}) collective-permute-start(bf16[192,1152]{1,0:T(8,128)(2,1)} %get-tuple-element.55), channel_id=1, source_target_pairs={{0,4},{2,6},{4,0},{6,2},{1,5},{3,7},{5,1},{7,3},{8,12},{10,14},{12... | collective-permute-start | bytes 1327112 | tf_op jit(solution)/shard_map/ppermute | solution.py:259
  347.0 14.4 %collective-permute-start.34 = (bf16[192,1152]{1,0:T(8,128)(2,1)S(1)}, bf16[192,1152]{1,0:T(8,128)(2,1)S(1)}, u32[]{:S(2)}, u32[]{:S(2)}) collective-permute-start(bf16[192,1152]{1,0:T(8,128)(2,1)S(1)} %get-tuple-element.54), channel_id=1, source_target_pairs={{0,2},{2,0},{4,6},{6,4},{1,3},{3,1},{5,7},{7,5},{8,10},{10,8},{12,... | collective-permute-start | bytes 1327112 | tf_op jit(solution)/shard_map/ppermute | solution.py:259
  360.6 24.5 %collective-permute-start.56 = (bf16[768,1536]{1,0:T(8,128)(2,1)S(1)}, bf16[768,1536]{1,0:T(8,128)(2,1)S(1)}, u32[]{:S(2)}, u32[]{:S(2)}) collective-permute-start(bf16[768,1536]{1,0:T(8,128)(2,1)S(1)} %slice.270), channel_id=1, source_target_pairs={{0,1},{1,0},{2,3},{3,2},{4,5},{5,4},{6,7},{7,6},{8,9},{9,8},{10,11... | collective-permute-start | bytes 7077896 | tf_op jit(solution)/shard_map/ppermute | solution.py:259
  361.6 15.7 %collective-permute-start.37 = (bf16[192,1152]{1,0:T(8,128)(2,1)S(1)}, bf16[192,1152]{1,0:T(8,128)(2,1)S(1)}, u32[]{:S(2)}, u32[]{:S(2)}) collective-permute-start(bf16[192,1152]{1,0:T(8,128)(2,1)S(1)} %add_convert_fusion.12), channel_id=1, source_target_pairs={{0,8},{24,16},{1,9},{25,17},{2,10},{26,18},{3,11},{27,19},{4,12},{... | collective-permute-start | bytes 1327112 | tf_op jit(solution)/shard_map/ppermute | solution.py:289
  367.8 11.0 %collective-permute-start.47 = (bf16[192,384]{1,0:T(8,128)(2,1)S(1)}, bf16[192,384]{1,0:T(8,128)(2,1)S(1)}, u32[]{:S(2)}, u32[]{:S(2)}) collective-permute-start(bf16[192,384]{1,0:T(8,128)(2,1)S(1)} %add_convert_fusion.15), channel_id=1, source_target_pairs={{8,0},{16,24},{9,1},{17,25},{10,2},{18,26},{11,3},{19,27},{12,4},{... | collective-permute-start | bytes 442376 | tf_op jit(solution)/shard_map/ppermute | solution.py:292
  378.8 30.6 %collective-permute-start.27 = (f32[1536]{0:T(1024)}, f32[1536]{0:T(1024)S(1)}, u32[]{:S(2)}, u32[]{:S(2)}) collective-permute-start(f32[1536]{0:T(1024)} %slice.210), channel_id=1, source_target_pairs={{0,1},{1,0},{2,3},{3,2},{4,5},{5,4},{6,7},{7,6},{8,9},{9,8},{10,11... | collective-permute-start | bytes 18440 | tf_op jit(solution)/shard_map/ppermute | solution.py:259
  379.6 13.4 %collective-permute-start.24 = (bf16[1024,1152]{1,0:T(8,128)(2,1)S(1)}, bf16[1024,1152]{1,0:T(8,128)(2,1)S(1)}, u32[]{:S(2)}, u32[]{:S(2)}) collective-permute-start(bf16[1024,1152]{1,0:T(8,128)(2,1)S(1)} %slice_bitcast_fusion), channel_id=1, source_target_pairs={{0,1},{1,0},{2,3},{3,2},{4,5},{5,4},{6,7},{7,6},{8,9},{9,8},{10,11... | collective-permute-start | bytes 7077896 | tf_op jit(solution)/shard_map/ppermute | solution.py:259
  380.3 48.6 %collective-permute-start.39 = (bf16[192,1152]{1,0:T(8,128)(2,1)S(1)}, bf16[192,1152]{1,0:T(8,128)(2,1)}, u32[]{:S(2)}, u32[]{:S(2)}) collective-permute-start(bf16[192,1152]{1,0:T(8,128)(2,1)S(1)} %add_convert_fusion.11), channel_id=1, source_target_pairs={{8,0},{16,24},{9,1},{17,25},{10,2},{18,26},{11,3},{19,27},{12,4},{... | collective-permute-start | bytes 1327112 | tf_op jit(solution)/shard_map/ppermute | solution.py:292
  386.5 18.5 %collective-permute-start.49 = (bf16[96,1536]{1,0:T(8,128)(2,1)}, bf16[96,1536]{1,0:T(8,128)(2,1)S(1)}, u32[]{:S(2)}, u32[]{:S(2)}) collective-permute-start(bf16[96,1536]{1,0:T(8,128)(2,1)} %get-tuple-element.52), channel_id=1, source_target_pairs={{0,4},{2,6},{4,0},{6,2},{1,5},{3,7},{5,1},{7,3},{8,12},{10,14},{12... | collective-permute-start | bytes 884744 | tf_op jit(solution)/shard_map/ppermute | solution.py:259
  391.9 14.1 %collective-permute-start.51 = (bf16[96,1536]{1,0:T(8,128)(2,1)}, bf16[96,1536]{1,0:T(8,128)(2,1)S(1)}, u32[]{:S(2)}, u32[]{:S(2)}) collective-permute-start(bf16[96,1536]{1,0:T(8,128)(2,1)} %get-tuple-element.53), channel_id=1, source_target_pairs={{0,2},{2,0},{4,6},{6,4},{1,3},{3,1},{5,7},{7,5},{8,10},{10,8},{12,... | collective-permute-start | bytes 884744 | tf_op jit(solution)/shard_map/ppermute | solution.py:259
  393.1 17.6 %collective-permute-start.57 = (bf16[96,1536]{1,0:T(8,128)(2,1)}, bf16[96,1536]{1,0:T(8,128)(2,1)S(1)}, u32[]{:S(2)}, u32[]{:S(2)}) collective-permute-start(bf16[96,1536]{1,0:T(8,128)(2,1)} %get-tuple-element.48), channel_id=1, source_target_pairs={{0,4},{2,6},{4,0},{6,2},{1,5},{3,7},{5,1},{7,3},{8,12},{10,14},{12... | collective-permute-start | bytes 884744 | tf_op jit(solution)/shard_map/ppermute | solution.py:259
  405.0 9.6 %collective-permute-start.59 = (bf16[96,1536]{1,0:T(8,128)(2,1)}, bf16[96,1536]{1,0:T(8,128)(2,1)S(1)}, u32[]{:S(2)}, u32[]{:S(2)}) collective-permute-start(bf16[96,1536]{1,0:T(8,128)(2,1)} %get-tuple-element.49), channel_id=1, source_target_pairs={{0,2},{2,0},{4,6},{6,4},{1,3},{3,1},{5,7},{7,5},{8,10},{10,8},{12,... | collective-permute-start | bytes 884744 | tf_op jit(solution)/shard_map/ppermute | solution.py:259
  407.8 48.7 %collective-permute-start.52 = (bf16[192,1536]{1,0:T(8,128)(2,1)S(1)}, bf16[192,1536]{1,0:T(8,128)(2,1)}, u32[]{:S(2)}, u32[]{:S(2)}) collective-permute-start(bf16[192,1536]{1,0:T(8,128)(2,1)S(1)} %get-tuple-element.51), channel_id=1, source_target_pairs={{0,4},{2,6},{4,0},{6,2},{1,5},{3,7},{5,1},{7,3},{8,12},{10,14},{12... | collective-permute-start | bytes 1769480 | tf_op jit(solution)/shard_map/ppermute | solution.py:259
  409.4 47.2 %collective-permute-start.50 = (bf16[192,1536]{1,0:T(8,128)(2,1)S(1)}, bf16[192,1536]{1,0:T(8,128)(2,1)S(1)}, u32[]{:S(2)}, u32[]{:S(2)}) collective-permute-start(bf16[192,1536]{1,0:T(8,128)(2,1)S(1)} %get-tuple-element.50), channel_id=1, source_target_pairs={{0,2},{2,0},{4,6},{6,4},{1,3},{3,1},{5,7},{7,5},{8,10},{10,8},{12,... | collective-permute-start | bytes 1769480 | tf_op jit(solution)/shard_map/ppermute | solution.py:259
  410.7 17.1 %collective-permute-start.28 = (f32[160,128]{1,0:T(8,128)S(1)}, f32[160,128]{1,0:T(8,128)S(1)}, u32[]{:S(2)}, u32[]{:S(2)}) collective-permute-start(f32[160,128]{1,0:T(8,128)S(1)} %pad_bitcast_fusion), channel_id=1, source_target_pairs={{0,2},{2,0},{4,6},{6,4},{1,3},{3,1},{5,7},{7,5},{8,10},{10,8},{12,... | collective-permute-start | bytes 245768 | tf_op jit(solution)/shard_map/ppermute | solution.py:259
  416.4 49.1 %collective-permute-start.60 = (bf16[192,1536]{1,0:T(8,128)(2,1)S(1)}, bf16[192,1536]{1,0:T(8,128)(2,1)S(1)}, u32[]{:S(2)}, u32[]{:S(2)}) collective-permute-start(bf16[192,1536]{1,0:T(8,128)(2,1)S(1)} %get-tuple-element.47), channel_id=1, source_target_pairs={{0,4},{2,6},{4,0},{6,2},{1,5},{3,7},{5,1},{7,3},{8,12},{10,14},{12... | collective-permute-start | bytes 1769480 | tf_op jit(solution)/shard_map/ppermute | solution.py:259
  427.9 37.7 %collective-permute-start.58 = (bf16[192,1536]{1,0:T(8,128)(2,1)S(1)}, bf16[192,1536]{1,0:T(8,128)(2,1)S(1)}, u32[]{:S(2)}, u32[]{:S(2)}) collective-permute-start(bf16[192,1536]{1,0:T(8,128)(2,1)S(1)} %get-tuple-element.46), channel_id=1, source_target_pairs={{0,2},{2,0},{4,6},{6,4},{1,3},{3,1},{5,7},{7,5},{8,10},{10,8},{12,... | collective-permute-start | bytes 1769480 | tf_op jit(solution)/shard_map/ppermute | solution.py:259
  428.9 9.1 %collective-permute-start.29 = (f32[160,128]{1,0:T(8,128)S(1)}, f32[160,128]{1,0:T(8,128)S(1)}, u32[]{:S(2)}, u32[]{:S(2)}) collective-permute-start(f32[160,128]{1,0:T(8,128)S(1)} %fusion.66), channel_id=1, source_target_pairs={{0,4},{2,6},{4,0},{6,2},{1,5},{3,7},{5,1},{7,3},{8,12},{10,14},{12... | collective-permute-start | bytes 245768 | tf_op jit(solution)/shard_map/ppermute | solution.py:259
  438.0 17.8 %collective-permute-start.30 = (f32[160,128]{1,0:T(8,128)S(1)}, f32[160,128]{1,0:T(8,128)S(1)}, u32[]{:S(2)}, u32[]{:S(2)}) collective-permute-start(f32[160,128]{1,0:T(8,128)S(1)} %fusion.86), channel_id=1, source_target_pairs={{0,8},{24,16},{1,9},{25,17},{2,10},{26,18},{3,11},{27,19},{4,12},{... | collective-permute-start | bytes 245768 | tf_op jit(solution)/shard_map/ppermute | solution.py:289
  458.2 19.7 %collective-permute-start.53 = (bf16[192,1536]{1,0:T(8,128)(2,1)S(1)}, bf16[192,1536]{1,0:T(8,128)(2,1)S(1)}, u32[]{:S(2)}, u32[]{:S(2)}) collective-permute-start(bf16[192,1536]{1,0:T(8,128)(2,1)S(1)} %add_convert_fusion.8), channel_id=1, source_target_pairs={{0,8},{24,16},{1,9},{25,17},{2,10},{26,18},{3,11},{27,19},{4,12},{... | collective-permute-start | bytes 1769480 | tf_op jit(solution)/shard_map/ppermute | solution.py:289
  467.1 20.8 %collective-permute-start.61 = (bf16[192,1536]{1,0:T(8,128)(2,1)S(1)}, bf16[192,1536]{1,0:T(8,128)(2,1)S(1)}, u32[]{:S(2)}, u32[]{:S(2)}) collective-permute-start(bf16[192,1536]{1,0:T(8,128)(2,1)S(1)} %add_convert_fusion.4), channel_id=1, source_target_pairs={{0,8},{24,16},{1,9},{25,17},{2,10},{26,18},{3,11},{27,19},{4,12},{... | collective-permute-start | bytes 1769480 | tf_op jit(solution)/shard_map/ppermute | solution.py:289
  478.1 11.2 %collective-permute-start.54 = (bf16[192,1536]{1,0:T(8,128)(2,1)S(1)}, bf16[192,1536]{1,0:T(8,128)(2,1)S(1)}, u32[]{:S(2)}, u32[]{:S(2)}) collective-permute-start(bf16[192,1536]{1,0:T(8,128)(2,1)S(1)} %fusion.45), channel_id=1, source_target_pairs={{8,16},{16,8},{9,17},{17,9},{10,18},{18,10},{11,19},{19,11},{12,20... | collective-permute-start | bytes 1769480 | tf_op jit(solution)/shard_map/ppermute | solution.py:291
  491.0 20.1 %collective-permute-start.55 = (bf16[192,1536]{1,0:T(8,128)(2,1)S(1)}, bf16[192,1536]{1,0:T(8,128)(2,1)S(1)}, u32[]{:S(2)}, u32[]{:S(2)}) collective-permute-start(bf16[192,1536]{1,0:T(8,128)(2,1)S(1)} %add_convert_fusion.7), channel_id=1, source_target_pairs={{8,0},{16,24},{9,1},{17,25},{10,2},{18,26},{11,3},{19,27},{12,4},{... | collective-permute-start | bytes 1769480 | tf_op jit(solution)/shard_map/ppermute | solution.py:292
  493.8 27.0 %collective-permute-start.63 = (bf16[192,1536]{1,0:T(8,128)(2,1)S(1)}, bf16[192,1536]{1,0:T(8,128)(2,1)S(1)}, u32[]{:S(2)}, u32[]{:S(2)}) collective-permute-start(bf16[192,1536]{1,0:T(8,128)(2,1)S(1)} %add_convert_fusion.3), channel_id=1, source_target_pairs={{8,0},{16,24},{9,1},{17,25},{10,2},{18,26},{11,3},{19,27},{12,4},{... | collective-permute-start | bytes 1769480 | tf_op jit(solution)/shard_map/ppermute | solution.py:292
  (80 other events, 896.4 us)

commit v2 on v1

v2 whole, which is shorter than its diff:
```python
import functools

import jax
import jax.numpy as jnp
from jax import lax
from jax.experimental import pallas as pl
from jax.experimental.pallas import tpu as pltpu
from jax.sharding import PartitionSpec as P

HEAD_DIM = 64
norm_eps = 1e-05
masked_score = -1000000000.0
low = jnp.bfloat16
wide = jnp.float32
tile_rows = 256


def cost(micros):
    return pl.CostEstimate(flops=int(micros * 1.1e9), transcendentals=0, bytes_accessed=1 << 20)


def dot_nn(left, right):
    return lax.dot_general(left, right, (((1,), (0,)), ((), ())), preferred_element_type=wide)


def dot_nt(left, right):
    return lax.dot_general(left, right, (((1,), (1,)), ((), ())), preferred_element_type=wide)


def dot_tn(left, right):
    return lax.dot_general(left, right, (((0,), (0,)), ((), ())), preferred_element_type=wide)


def column_of(ids_row):
    parts = []
    for start in range(0, ids_row.shape[1], 128):
        piece = ids_row[:, start : start + 128].astype(wide)
        parts.append(jnp.transpose(jnp.broadcast_to(piece, (128, 128))))
    return jnp.concatenate(parts, axis=0)


def lanes(values):
    return [values[:, first : first + 128] for first in range(0, values.shape[1], 128)]


def variants(count):
    return [(2 * n, min(2 * n + 3, count)) for n in range(count // 2)]


def key_tile(ref, tile, half, side):
    rows = slice((tile % half) * tile_rows, (tile % half + 1) * tile_rows)
    return ref[(tile // half) ^ side, rows, :]


def allowed_part(ids_ref, ids_column, first):
    return ids_ref[:, first : first + 128].astype(wide) <= ids_column


def row_tile(half, shift):
    return lambda i, c: jnp.clip(i - half * (c[0] ^ shift), 0, half - 1)


def attend_forward_body(
    count, half, col_ref, q_ref, k_ref, v_ref, ids_ref, own_ref, other_ref, lse_ref, s_ref
):
    step, head = pl.program_id(1), pl.program_id(2)
    side = col_ref[0]
    lane = lax.broadcasted_iota(jnp.int32, (tile_rows, 128), 1)
    mine = lane // HEAD_DIM == head
    own_ids = ids_ref[:, pl.ds(pl.multiple_of(step * tile_rows, tile_rows), tile_rows)]

    def variant(open_tiles, keys):
        query = q_ref[...]
        part = jnp.where(mine, query, jnp.zeros_like(query)) * jnp.asarray(0.125, low)
        ids_column = column_of(own_ids)
        top = None
        for tile in range(keys):
            first = tile * tile_rows
            scores = lanes(dot_nt(part, key_tile(k_ref, tile, half, side)))
            for n, values in enumerate(scores):
                at = first + 128 * n
                if tile >= open_tiles:
                    values = jnp.where(
                        allowed_part(ids_ref, ids_column, at), values, masked_score
                    )
                s_ref[:, at : at + 128] = values
                top = values if top is None else jnp.maximum(top, values)
        top = jnp.max(top, axis=1, keepdims=True)
        total = None
        acc = None
        for tile in range(keys):
            first = tile * tile_rows
            expo = [jnp.exp(s - top) for s in lanes(s_ref[:, first : first + tile_rows])]
            for values in expo:
                total = values if total is None else total + values
            low_expo = jnp.concatenate([e.astype(low) for e in expo], axis=1)
            mixed = dot_nn(low_expo, key_tile(v_ref, tile, half, side))
            acc = mixed if acc is None else acc + mixed
        total = jnp.sum(total, axis=1, keepdims=True)
        out = (acc / total).astype(low)
        lse_ref[...] = jnp.where(
            lax.broadcasted_iota(jnp.int32, lse_ref.shape, 1) == head,
            top + jnp.log(total),
            lse_ref[...],
        )
        owned = (step // half) ^ side == 0

        @pl.when(owned)
        def _():
            own_ref[...] = jnp.where(mine, out, own_ref[...])

        @pl.when(jnp.logical_not(owned))
        def _():
            other_ref[...] = jnp.where(mine, out, other_ref[...])

    for n, bounds in enumerate(variants(count)):
        pl.when(step // 2 == n)(functools.partial(variant, *bounds))


def attend_forward(meta, qkv, ids, first, pairs):
    sides, rows, _ = qkv.shape
    length = sides * rows
    count = length // tile_rows
    half = rows // tile_rows
    head_cols = 128 * pairs
    own, other = row_tile(half, 0), row_tile(half, 1)
    return pl.pallas_call(
        functools.partial(attend_forward_body, count, half),
        grid_spec=pltpu.PrefetchScalarGridSpec(
            num_scalar_prefetch=1,
            grid=(pairs, count, 2),
            in_specs=[
                pl.BlockSpec(
                    (None, tile_rows, 128),
                    lambda h, i, e, c: ((i // half) ^ c[0], i % half, 3 * (h + first)),
                ),
                pl.BlockSpec((sides, rows, 128), lambda h, i, e, c: (0, 0, 3 * (h + first) + 1)),
                pl.BlockSpec((sides, rows, 128), lambda h, i, e, c: (0, 0, 3 * (h + first) + 2)),
                pl.BlockSpec((1, length), lambda h, i, e, c: (0, 0)),
            ],
            out_specs=[
                pl.BlockSpec((tile_rows, 128), lambda h, i, e, c: (own(i, c), h)),
                pl.BlockSpec((tile_rows, 128), lambda h, i, e, c: (other(i, c), h)),
                pl.BlockSpec((None, tile_rows, 2), lambda h, i, e, c: (h, i, 0)),
            ],
            scratch_shapes=[pltpu.VMEM((tile_rows, length), wide)],
        ),
        out_shape=[
            jax.ShapeDtypeStruct((rows, head_cols), low),
            jax.ShapeDtypeStruct((rows, head_cols), low),
            jax.ShapeDtypeStruct((pairs, length, 2), wide),
        ],
        cost_estimate=cost(14 * pairs),
        name="attend_forward",
    )(meta, qkv, qkv, qkv, ids)


def attend_backward_body(
    count, half, col_ref, q_ref, k_ref, v_ref, g_ref, g_other_ref, ids_ref, lse_ref,
    own_ref, other_ref, sum_ref, p_ref, gp_ref, low_ref, gq_ref, gk_acc, gv_acc,
):
    step, head = pl.program_id(1), pl.program_id(2)
    side = col_ref[0]
    lane = lax.broadcasted_iota(jnp.int32, (tile_rows, 128), 1)
    mine = lane // HEAD_DIM == head
    own_ids = ids_ref[:, pl.ds(pl.multiple_of(step * tile_rows, tile_rows), tile_rows)]

    def store(tile, place, values):
        start = pl.multiple_of((tile % half) * tile_rows, tile_rows)
        here = (pl.ds(start, tile_rows), slice(place * 128, (place + 1) * 128))
        owned = (tile // half) ^ side == 0

        @pl.when(owned)
        def _():
            own_ref[here] = values

        @pl.when(jnp.logical_not(owned))
        def _():
            other_ref[here] = values

    @pl.when((step == 0) & (head == 0))
    def _():
        gk_acc[...] = jnp.zeros_like(gk_acc)
        gv_acc[...] = jnp.zeros_like(gv_acc)
        sum_ref[...] = jnp.zeros_like(sum_ref)

    def variant(open_tiles, keys):
        query = q_ref[...]
        grad = jnp.where((step // half) ^ side == 0, g_ref[...], g_other_ref[...])
        part = jnp.where(mine, query, jnp.zeros_like(query)) * jnp.asarray(0.125, low)
        grad_part = jnp.where(mine, grad, jnp.zeros_like(grad))
        start = pl.multiple_of(head * HEAD_DIM, HEAD_DIM)
        spot = pl.ds(start, HEAD_DIM)

        def turned(values):
            flat = jnp.transpose(values)
            return jnp.where(head == 0, flat[:HEAD_DIM], flat[HEAD_DIM:])

        query_turned, grad_turned = turned(query), turned(grad)
        ids_column = column_of(own_ids)
        log_sum = jnp.where(head == 0, lse_ref[:, :1], lse_ref[:, 1:])
        inner = None
        for tile in range(keys):
            first = tile * tile_rows
            here = slice(first, first + tile_rows)
            scores = lanes(dot_nt(part, key_tile(k_ref, tile, half, side)))
            grad_probs = dot_nt(grad_part, key_tile(v_ref, tile, half, side))
            gp_ref[:, here] = grad_probs
            lows = []
            for n, (values, slope) in enumerate(zip(scores, lanes(grad_probs))):
                at = first + 128 * n
                values = jnp.exp(values - log_sum)
                if tile >= open_tiles:
                    values = jnp.where(allowed_part(ids_ref, ids_column, at), values, 0.0)
                p_ref[:, at : at + 128] = values
                lows.append(values.astype(low))
                values = values * slope
                inner = values if inner is None else inner + values
            lows = jnp.concatenate(lows, axis=1)
            gv_acc[spot, here] += dot_nn(grad_turned, lows)
        inner = jnp.sum(inner, axis=1, keepdims=True)
        grad_query = None
        for tile in range(keys):
            here = slice(tile * tile_rows, (tile + 1) * tile_rows)
            slopes = (p_ref[:, here] * (gp_ref[:, here] - inner)).astype(low)
            piece = dot_nn(slopes, key_tile(k_ref, tile, half, side))
            grad_query = piece if grad_query is None else grad_query + piece
            gk_acc[spot, here] += dot_nn(query_turned, slopes)
        gq_ref[...] = jnp.where(mine, grad_query, gq_ref[...])

    for n, bounds in enumerate(variants(count)):
        pl.when(step // 2 == n)(functools.partial(variant, *bounds))

    @pl.when(head == 1)
    def _():
        out = (gq_ref[...] * 0.125).astype(low)
        store(step, 0, out)
        sum_ref[0:1, :] += jnp.sum(out.astype(wide), axis=0, keepdims=True)

    @pl.when((step == count - 1) & (head == 1))
    def _():
        def finish(tile, _):
            here = pl.ds(pl.multiple_of(tile * tile_rows, tile_rows), tile_rows)
            grad_key = jnp.transpose(gk_acc[:, here] * 0.125).astype(low)
            grad_value = jnp.transpose(gv_acc[:, here]).astype(low)
            store(tile, 1, grad_key)
            store(tile, 2, grad_value)
            sum_ref[1:2, :] += jnp.sum(grad_value.astype(wide), axis=0, keepdims=True)

        lax.fori_loop(0, count, finish, None)


def attend_backward(meta, qkv, grad, grad_other, ids, log_sums, first, pairs, lse_first):
    sides, rows, _ = qkv.shape
    length = sides * rows
    count = length // tile_rows
    half = rows // tile_rows
    own, other = row_tile(half, 0), row_tile(half, 1)
    whole = pl.BlockSpec((rows, 384), lambda h, i, e, c: (0, h))
    return pl.pallas_call(
        functools.partial(attend_backward_body, count, half),
        grid_spec=pltpu.PrefetchScalarGridSpec(
            num_scalar_prefetch=1,
            grid=(pairs, count, 2),
            in_specs=[
                pl.BlockSpec(
                    (None, tile_rows, 128),
                    lambda h, i, e, c: ((i // half) ^ c[0], i % half, 3 * (h + first)),
                ),
                pl.BlockSpec((sides, rows, 128), lambda h, i, e, c: (0, 0, 3 * (h + first) + 1)),
                pl.BlockSpec((sides, rows, 128), lambda h, i, e, c: (0, 0, 3 * (h + first) + 2)),
                pl.BlockSpec((tile_rows, 128), lambda h, i, e, c: (own(i, c), h + first)),
                pl.BlockSpec((tile_rows, 128), lambda h, i, e, c: (other(i, c), h + first)),
                pl.BlockSpec((1, length), lambda h, i, e, c: (0, 0)),
                pl.BlockSpec((None, tile_rows, 2), lambda h, i, e, c: (h + lse_first, i, 0)),
            ],
            out_specs=[whole, whole, pl.BlockSpec((8, 128), lambda h, i, e, c: (0, h))],
            scratch_shapes=[
                pltpu.VMEM((tile_rows, length), wide),
                pltpu.VMEM((tile_rows, length), wide),
                pltpu.VMEM((8, 128), low),
                pltpu.VMEM((tile_rows, 128), wide),
                pltpu.VMEM((128, length), wide),
                pltpu.VMEM((128, length), wide),
            ],
        ),
        out_shape=[jax.ShapeDtypeStruct((rows, 384 * pairs), low)] * 2
        + [jax.ShapeDtypeStruct((8, 128 * pairs), wide)],
        cost_estimate=cost(25 * pairs),
        name="attend_backward",
    )(meta, qkv, qkv, qkv, grad, grad_other, ids, log_sums)


def norm_parts(values):
    mean = jnp.mean(values, axis=-1, keepdims=True)
    centred = values - mean
    inverse = lax.rsqrt(jnp.mean(centred * centred, axis=-1, keepdims=True) + norm_eps)
    return centred * inverse, inverse


def norm_back(grad_normed, unit, inverse, gain):
    grad_unit = grad_normed * gain
    first_mean = jnp.mean(grad_unit, axis=-1, keepdims=True)
    second_mean = jnp.mean(grad_unit * unit, axis=-1, keepdims=True)
    return inverse * (grad_unit - first_mean - unit * second_mean)


erfc_terms = (
    -0.12664913241116757, 0.4719797697046255, -0.4849989149703286, 0.5173882238837517,
    -0.0742751946996765, 0.20647784419749105, 0.15044607588806108, 0.17042678586105697,
    0.16920458065681523,
)


def gelu_with_slope(values):
    turned = 1.0 / (1.0 + (0.3 * 0.5**0.5) * jnp.abs(values))
    bell = jnp.exp(-0.5 * (values * values))
    series = jnp.full_like(values, 0.5 * erfc_terms[0])
    for term in erfc_terms[1:]:
        series = series * turned + 0.5 * term
    tail = series * turned * bell
    below = jnp.where(values < 0.0, tail, 1.0 - tail)
    return values * below, below + values * (bell * (0.5 / jnp.pi) ** 0.5)


def swap(values, axis, distance):
    size = lax.axis_size(axis)
    return lax.ppermute(values, axis, [(i, i ^ distance) for i in range(size)])


def gather_near(shard):
    return swap(shard, "row", 1), swap(shard, "row", 2)


def gather_far(shard, from_x, from_y):
    cut = shard.shape[0] // 2
    first_xy = swap(from_x[:cut], "row", 2)
    second_xy = swap(from_y[cut:], "row", 1)
    return [(0, 0, shard), (1, 0, from_x), (2, 0, from_y), (3, 0, first_xy), (3, cut, second_xy)]


def piece_copies(layout, refs, target, row_index, shard_rows, sems):
    copies = []
    for n, ((distance, first, rows), ref) in enumerate(zip(layout, refs)):
        base = pl.multiple_of((row_index ^ distance) * shard_rows + first, 16)
        copies.append(pltpu.make_async_copy(ref, target.at[pl.ds(base, rows), :], sems.at[n]))
    return copies


def layout_of(pieces):
    return [(distance, first, piece.shape[0]) for distance, first, piece in pieces]


hbm = pl.BlockSpec(memory_space=pl.ANY)


def project_in_body(layout, tiles, meta_ref, mine_ref, other_ref, bias_ref, *rest):
    pieces = rest[: len(layout)]
    out_ref, turned_ref, weight_out, weight, sems, out_sem = rest[len(layout) :]
    step = pl.program_id(0)
    keep = pltpu.make_async_copy(weight, weight_out, out_sem)

    @pl.when(step == 0)
    def _():
        copies = piece_copies(layout, pieces, weight, meta_ref[1], weight.shape[0] // 4, sems)
        for copy in copies:
            copy.start()
        for copy in copies:
            copy.wait()
        keep.start()

    @pl.when(step < tiles)
    def _():
        rows = mine_ref[...]
        out_ref[...] = (dot_nn(rows, weight[...]) + bias_ref[...]).astype(low)
        turned_ref[...] = jnp.transpose(rows)

    @pl.when(step >= tiles)
    def _():
        rows = other_ref[...]
        out_ref[...] = (dot_nn(rows, weight[...]) + bias_ref[...]).astype(low)
        turned_ref[...] = jnp.transpose(rows)

    @pl.when(step == 2 * tiles - 1)
    def _():
        keep.wait()


def project_in(meta, mine, other, bias, pieces):
    rows, model = mine.shape
    size = 2 * tile_rows
    tiles = rows // size
    width = pieces[0][2].shape[1]
    return pl.pallas_call(
        functools.partial(project_in_body, layout_of(pieces), tiles),
        grid_spec=pltpu.PrefetchScalarGridSpec(
            num_scalar_prefetch=1,
            grid=(2 * tiles,),
            in_specs=[
                pl.BlockSpec((size, model), lambda i, m: (jnp.minimum(i, tiles - 1), 0)),
                pl.BlockSpec((size, model), lambda i, m: (jnp.maximum(i - tiles, 0), 0)),
                pl.BlockSpec((1, width), lambda i, m: (0, 0)),
            ]
            + [hbm] * len(pieces),
            out_specs=[
                pl.BlockSpec((None, size, width), lambda i, m: (i // tiles, i % tiles, 0)),
                pl.BlockSpec((model, size), lambda i, m: (0, i)),
                hbm,
            ],
            scratch_shapes=[
                pltpu.VMEM((model, width), low),
                pltpu.SemaphoreType.DMA((len(pieces),)),
                pltpu.SemaphoreType.DMA(()),
            ],
        ),
        out_shape=[
            jax.ShapeDtypeStruct((2, rows, width), low),
            jax.ShapeDtypeStruct((model, 2 * rows), low),
            jax.ShapeDtypeStruct((model, width), low),
        ],
        cost_estimate=cost(7),
        name="project_in",
    )(meta, mine, other, bias, *[piece for _, _, piece in pieces])


def load_weights(layout, pieces, weight, meta_ref, sems):
    copies = []
    for side in range(2):
        copies += piece_copies(
            layout, pieces[side], weight.at[side], meta_ref[1], weight.shape[1] // 4, sems.at[side]
        )
    for copy in copies:
        copy.start()
    for copy in copies:
        copy.wait()


hidden_chunk = 512


def feed_body(
    layout, head_cols, hidden_cols, meta_ref, tok_ref, row_ref, mixed_ref, mixed_last_ref,
    got_ref, got_last_ref, cot_ref, vec_ref, up_bias_ref, *rest,
):
    count = len(layout)
    pieces = (rest[:count], rest[count : 2 * count])
    (
        out_ref, keep_ref, send_ref, gkeep_ref, gsend_ref, two_ref, cot_turned_ref, branch_ref,
        middle_ref, own_ref, other_ref, sum_ref, bias_ref, weight, sems,
    ) = rest[2 * count :]

    @pl.when(pl.program_id(0) == 0)
    def _():
        load_weights(layout, pieces, weight, meta_ref, sems)
        sum_ref[...] = jnp.zeros_like(sum_ref)
        bias_ref[...] = jnp.zeros_like(bias_ref)

    bias_out, gain, bias, bias_down = (vec_ref[n : n + 1, :] for n in range(4))
    cot = cot_ref[...]
    cot_turned_ref[...] = jnp.transpose(cot)
    start = tok_ref[...].astype(wide) + row_ref[...]
    cut = mixed_ref.shape[1]
    branch = dot_nt(mixed_ref[...], weight[0, :, :cut])
    branch = branch + dot_nt(mixed_last_ref[...], weight[0, :, cut:head_cols])
    branch = branch + dot_nt(got_ref[...], weight[1, :, :cut])
    branch = branch + dot_nt(got_last_ref[...], weight[1, :, cut:head_cols])
    middle = start + (branch + bias_out)
    unit, inverse = norm_parts(middle)
    two = (unit * gain + bias).astype(low)
    two_ref[...] = jnp.transpose(two)
    mixer = None
    grad_two = None
    for side in range(2):
        for first in range(0, hidden_cols, hidden_chunk):
            here = slice(first, first + hidden_chunk)
            there = slice(side * hidden_cols + first, side * hidden_cols + first + hidden_chunk)
            up = weight[side, :, head_cols + first : head_cols + first + hidden_chunk]
            at = head_cols + hidden_cols + first
            down = weight[side, :, at : at + hidden_chunk]
            hidden, slope = gelu_with_slope(dot_nn(two, up) + up_bias_ref[:, there])
            hidden = hidden.astype(low)
            (send_ref if side else keep_ref)[:, here] = hidden
            part = dot_nt(hidden, down)
            mixer = part if mixer is None else mixer + part
            grad_pre = (dot_nn(cot, down) * slope).astype(low)
            (gsend_ref if side else gkeep_ref)[:, here] = grad_pre
            bias_ref[:, there] += jnp.sum(grad_pre.astype(wide), axis=0, keepdims=True)
            part = dot_nt(grad_pre, up)
            grad_two = part if grad_two is None else grad_two + part
    out_ref[...] = (middle + (mixer + bias_down)).astype(low)
    cot = cot.astype(wide)
    grad_middle = cot + norm_back(grad_two, unit, inverse, gain)
    grad_branch = grad_middle.astype(low)
    middle_ref[...] = grad_middle
    branch_ref[...] = jnp.transpose(grad_branch)
    own_ref[...] = dot_nn(grad_branch, weight[0, :, :head_cols]).astype(low)
    other_ref[...] = dot_nn(grad_branch, weight[1, :, :head_cols]).astype(low)
    for n, values in enumerate((grad_branch.astype(wide), grad_two * unit, grad_two, cot)):
        sum_ref[n : n + 1, :] += jnp.sum(values, axis=0, keepdims=True)


def feed(meta, tokens, table_row, mixed, got, cot, vectors, up_bias, mine, other):
    rows, model = tokens.shape
    size = tile_rows
    head_cols = sum(part.shape[1] for part in mixed)
    hidden_cols = up_bias.shape[1] // 2
    width = mine[0][2].shape[1]

    def tile(columns):
        return pl.BlockSpec((size, columns), lambda i, m: (i, 0))

    def fixed(*shape):
        return pl.BlockSpec(shape, lambda i, m: (0,) * len(shape))

    def turned(depth):
        return pl.BlockSpec((depth, size), lambda i, m: (0, i))

    def array(columns, dtype):
        return jax.ShapeDtypeStruct((rows, columns), dtype)

    flipped = jax.ShapeDtypeStruct((model, rows), low)
    return pl.pallas_call(
        functools.partial(feed_body, layout_of(mine), head_cols, hidden_cols),
        grid_spec=pltpu.PrefetchScalarGridSpec(
            num_scalar_prefetch=1,
            grid=(rows // size,),
            in_specs=[tile(model), fixed(1, model)]
            + [tile(part.shape[1]) for part in (*mixed, *got)]
            + [tile(model), fixed(8, model), fixed(1, 2 * hidden_cols)]
            + [hbm] * (2 * len(mine)),
            out_specs=[tile(model)]
            + [tile(hidden_cols)] * 4
            + [turned(model)] * 3
            + [tile(model), tile(head_cols), tile(head_cols), fixed(8, model)]
            + [fixed(1, 2 * hidden_cols)],
            scratch_shapes=[
                pltpu.VMEM((2, model, width), low),
                pltpu.SemaphoreType.DMA((2, len(mine))),
            ],
        ),
        out_shape=[array(model, low)]
        + [array(hidden_cols, low)] * 4
        + [flipped] * 3
        + [array(model, wide), array(head_cols, low), array(head_cols, low)]
        + [jax.ShapeDtypeStruct((8, model), wide)]
        + [jax.ShapeDtypeStruct((1, 2 * hidden_cols), wide)],
        cost_estimate=cost(45),
        name="feed",
    )(
        meta, tokens, table_row, *mixed, *got, cot, vectors, up_bias,
        *[piece for _, _, piece in mine], *[piece for _, _, piece in other],
    )


def weight_parts_body(products, near, meta_ref, *refs):
    send_ref, keep_ref = refs[-2:]
    shard = send_ref.shape[0] // 2
    order = [pl.multiple_of((meta_ref[1] ^ d) * shard, 64) for d in (3, near, 3 - near, 0)]

    def in_order(ref):
        return jnp.concatenate([ref[pl.ds(start, shard), :] for start in order], axis=0)

    at = 0
    for lefts, arrived, first, tiles in products:
        inputs = refs[at : at + 2 * lefts + arrived]
        at += 2 * lefts + arrived

        @pl.when((pl.program_id(0) >= first) & (pl.program_id(0) < first + tiles))
        def _(inputs=inputs, lefts=lefts, arrived=arrived):
            total = None
            for n in range(lefts):
                part = dot_nn(in_order(inputs[2 * n]), inputs[2 * n + 1][...])
                total = part if total is None else total + part
            if arrived:
                total = total + in_order(inputs[-1]).astype(wide)
            total = total.astype(low)
            send_ref[...] = total[: 2 * shard]
            keep_ref[...] = total[2 * shard :]


def weight_parts(meta, products, near, micros):
    model = products[0][0][0][0].shape[0]
    operands, specs, shapes = [], [], []
    step = 384
    first = 0
    for pairs, arrived in products:
        tiles = pairs[0][2].shape[1] // step

        def tile(i, m, first=first, tiles=tiles):
            return (0, jnp.clip(i - first, 0, tiles - 1))

        for left, place, right in pairs:
            depth = right.shape[0]
            specs.append(pl.BlockSpec((model, depth), lambda i, m, p=place: (0, p)))
            specs.append(pl.BlockSpec((depth, step), tile))
            operands += [left, right]
        if arrived is not None:
            specs.append(pl.BlockSpec((model, step), tile))
            operands.append(arrived)
        shapes.append((len(pairs), int(arrived is not None), first, tiles))
        first += tiles
    half = jax.ShapeDtypeStruct((model // 2, first * step), low)
    return pl.pallas_call(
        functools.partial(weight_parts_body, shapes, near),
        grid_spec=pltpu.PrefetchScalarGridSpec(
            num_scalar_prefetch=1,
            grid=(first,),
            in_specs=specs,
            out_specs=[pl.BlockSpec((model // 2, step), lambda i, m: (0, i))] * 2,
        ),
        out_shape=[half, half],
        cost_estimate=cost(micros),
        name="weight_parts",
    )(meta, *operands)


def product_body(left_ref, right_ref, out_ref):
    out_ref[...] = dot_nn(left_ref[...], right_ref[...]).astype(low)


def product(left, right, micros):
    rows, depth = left.shape
    columns = right.shape[1]
    step = 384
    return pl.pallas_call(
        product_body,
        grid=(columns // step,),
        in_specs=[
            pl.BlockSpec((rows, depth), lambda i: (0, 0)),
            pl.BlockSpec((depth, step), lambda i: (0, i)),
        ],
        out_specs=pl.BlockSpec((rows, step), lambda i: (0, i)),
        out_shape=jax.ShapeDtypeStruct((rows, columns), low),
        cost_estimate=cost(micros),
        name="product",
    )(left, right)


def pack_body(*refs):
    out_ref = refs[-1]
    for n in range(out_ref.shape[1] // 128):
        kind, pair = n % 3, n // 3
        out_ref[:, 128 * n : 128 * (n + 1)] = refs[kind][:, 128 * pair : 128 * (pair + 1)].astype(low)


def pack(*weights):
    rows, columns = weights[0].shape
    return pl.pallas_call(
        pack_body,
        out_shape=jax.ShapeDtypeStruct((rows, 3 * columns), low),
        cost_estimate=cost(1),
        name="pack",
    )(*weights)


def grad_in_body(cuts, tok_ref, row_ref, gain_ref, own_ref, other_ref, middle_ref, *rest):
    grads = rest[: 2 * len(cuts)]
    out_ref, sum_ref = rest[2 * len(cuts) :]

    @pl.when(pl.program_id(0) == 0)
    def _():
        sum_ref[...] = jnp.zeros_like(sum_ref)

    grad = None
    for n, (first, last) in enumerate(cuts):
        for values, weight in ((grads[2 * n], own_ref), (grads[2 * n + 1], other_ref)):
            part = dot_nt(values[...], weight[:, first:last])
            grad = part if grad is None else grad + part
    unit, inverse = norm_parts(tok_ref[...].astype(wide) + row_ref[...])
    tokens = middle_ref[...] + norm_back(grad, unit, inverse, gain_ref[...])
    out_ref[...] = tokens
    for n, values in enumerate((grad * unit, grad, tokens)):
        sum_ref[n : n + 1, :] += jnp.sum(values, axis=0, keepdims=True)


def grad_in(tokens, table_row, gain, own, other, grad_middle, grads):
    rows, model = tokens.shape
    size = tile_rows
    width = own.shape[1]
    cuts = []
    for mine, _ in grads:
        first = cuts[-1][1] if cuts else 0
        cuts.append((first, first + mine.shape[1]))

    def tile(columns):
        return pl.BlockSpec((size, columns), lambda i: (i, 0))

    def fixed(*shape):
        return pl.BlockSpec(shape, lambda i: (0, 0))

    flat = [values for pair in grads for values in pair]
    return pl.pallas_call(
        functools.partial(grad_in_body, cuts),
        grid=(rows // size,),
        in_specs=[
            tile(model), fixed(1, model), fixed(1, model), fixed(model, width),
            fixed(model, width), tile(model),
        ]
        + [tile(values.shape[1]) for values in flat],
        out_specs=[tile(model), fixed(8, model)],
        out_shape=[
            jax.ShapeDtypeStruct((rows, model), wide),
            jax.ShapeDtypeStruct((8, model), wide),
        ],
        cost_estimate=cost(9),
        name="grad_in",
    )(tokens, table_row, gain, own, other, grad_middle, *flat)


def after(values, *needed):
    needed = [value for value in needed if value is not None]
    return lax.optimization_barrier((values, *needed))[0] if needed else values


def line_steps(values):
    if lax.axis_size("dp") != 4:
        return lax.psum(values, "dp")
    for distance in (1, 2):
        arrived = swap(values, "dp", distance)
        token = yield values
        arrived = after(arrived, token)
        values = (values.astype(wide) + arrived.astype(wide)).astype(values.dtype)
    return values


def weight_steps(parts, near):
    send, keep = parts
    shard = send.shape[0] // 2
    arrived = swap(send, "row", near)
    token = yield send
    arrived = after(arrived, token)
    passed = (keep[:shard].astype(wide) + arrived[:shard].astype(wide)).astype(low)
    last = swap(passed, "row", 3 - near)
    token = yield passed
    last = after(last, token)
    share = keep[shard:].astype(wide) + arrived[shard:].astype(wide) + last.astype(wide)
    total = yield from line_steps(share.astype(low))
    return total.astype(wide)


def vector_steps(values):
    for axis, distance in (("row", 1), ("row", 2)):
        arrived = swap(values, axis, distance)
        token = yield values
        values = values + after(arrived, token)
    total = yield from line_steps(values)
    return total


class Chains:
    def __init__(self):
        self.steps, self.done = [], {}

    def add(self, steps):
        self.steps.append(steps)
        return [next(steps)]

    def advance(self, token=None, chosen=None):
        sent = []
        for n, steps in enumerate(self.steps):
            if n not in self.done and (chosen is None or n in chosen):
                try:
                    sent.append(steps.send(token))
                except StopIteration as stop:
                    self.done[n] = stop.value
        return sent


def shards(
    tokens, timesteps, block_ids, table, gain_one, bias_one, w_query, w_key, w_value, b_query,
    b_value, w_out, b_out, gain_two, bias_two, w_up, b_up, w_down, b_down, cotangent,
):
    seq_count, local_len, model_width = tokens.shape
    row_size, dp_size = lax.axis_size("row"), lax.axis_size("dp")
    assert seq_count == 1 and lax.axis_size("col") == 2 and row_size == 4
    head_cols = w_query.shape[1]
    hidden_cols = w_up.shape[1]
    col_index = lax.axis_index("col")
    row_index = lax.axis_index("row")
    seq_index = lax.axis_index("dp") * row_size + row_index
    seq_total = dp_size * row_size
    meta = jnp.stack([col_index, row_index]).astype(jnp.int32)

    cuts = [slice(first, first + 128) for first in range(0, head_cols, 128)]
    group_one = pack(w_query, w_key, w_value)
    in_bias = jnp.concatenate(
        [part for cut in cuts for part in (b_query[cut], jnp.zeros_like(b_query[cut]), b_value[cut])]
    )[None]
    in_pieces = gather_far(group_one, *gather_near(group_one))
    group_two = jnp.concatenate([w_out.T, w_up, w_down.T], axis=1).astype(low)
    group_two = after(group_two, in_pieces[3][2], in_pieces[4][2])
    near_x, near_y = gather_near(group_two)

    table_row = lax.dynamic_slice_in_dim(table, timesteps[0], 1, 0)
    unit_one, _ = norm_parts(tokens[0].astype(wide) + table_row)
    rows_mine = (unit_one * gain_one + bias_one).astype(low)
    rows_other = swap(rows_mine, "col", 1)
    up_bias = jnp.concatenate([b_up, swap(b_up, "col", 1)])[None]
    qkv, rows_turned, in_own = project_in(
        meta, rows_mine, after(rows_other, up_bias), in_bias, in_pieces
    )
    in_other = swap(in_own, "col", 1)
    shard_other = swap(group_two, "col", 1)
    pairs = head_cols // 128
    mixed, mixed_other, log_sums = attend_forward(
        meta, after(qkv, in_other, shard_other), block_ids, 0, pairs - 1
    )
    got = swap(mixed_other, "col", 1)
    near_x, near_y = after(near_x, mixed), after(near_y, mixed)
    near_x_other, near_y_other = swap(near_x, "col", 1), swap(near_y, "col", 1)
    mine = gather_far(group_two, near_x, near_y)
    mixed_last, mixed_last_other, log_sums_last = attend_forward(
        meta, after(qkv, got, near_x_other, near_y_other), block_ids, pairs - 1, 1
    )
    got_last = swap(mixed_last_other, "col", 1)
    far = [after(piece, mixed_last) for _, _, piece in mine[3:]]
    others = [shard_other, near_x_other, near_y_other] + [swap(piece, "col", 1) for piece in far]
    other = [(distance, first, piece) for (distance, first, _), piece in zip(mine, others)]

    spare = jnp.zeros_like(b_out)
    vectors = jnp.stack([b_out, gain_two, bias_two, b_down, spare, spare, spare, spare])
    cot = cotangent[0]
    (
        layer_out, keep, send, grad_keep, grad_send, two_turned, cot_turned, branch_turned,
        grad_middle, grad_own, grad_other, sums, grad_up_bias,
    ) = feed(
        meta, tokens[0], table_row, (mixed, mixed_last), (got, got_last), cot, vectors, up_bias,
        mine, other,
    )
    up_arrived = swap(product(two_turned, grad_send, 4), "col", 1)
    out_arrived = swap(
        product(branch_turned, jnp.concatenate([got, got_last], axis=1), 1), "col", 1
    )
    down_arrived = swap(product(cot_turned, send, 4), "col", 1)
    grad_got = swap(grad_other, "col", 1)
    up_parts = weight_parts(
        meta,
        [
            ([(two_turned, 0, grad_keep)], up_arrived),
            ([(branch_turned, 0, jnp.concatenate([mixed, mixed_last], axis=1))], out_arrived),
        ],
        1,
        8,
    )
    chains = Chains()
    chains.add(weight_steps(up_parts, 1))
    down_parts = weight_parts(
        meta, [([(cot_turned, 0, after(keep, *up_parts))], down_arrived)], 2, 7
    )
    chains.add(weight_steps(down_parts, 2))
    grad_b_up = grad_up_bias[0, :hidden_cols] + swap(grad_up_bias[0, hidden_cols:], "col", 1)
    before = [*up_parts, *down_parts, grad_b_up]

    own_grads, gots, bias_sums = [], [], []
    for pair in range(pairs):
        last = pair == pairs - 1
        own, away, bias_sum = attend_backward(
            meta, after(qkv, *before), grad_own, grad_got, block_ids,
            log_sums_last if last else log_sums, pair, 1, 0 if last else pair,
        )
        own_grads.append(own)
        gots.append(swap(away, "col", 1))
        bias_sums.append(bias_sum)
        before = [*chains.advance(own), gots[-1]]
        if last or pair == pairs - 2:
            products = [(own, away)] if last else list(zip(own_grads, aways + [away]))
            near = 1 if last else 2
            parts = weight_parts(
                meta,
                [([(rows_turned, 0, a), (rows_turned, 1, b)], None) for a, b in products],
                near,
                3 * len(products),
            )
            before += parts
            chains.add(weight_steps(parts, near))
        else:
            aways = [away] if pair == 0 else aways + [away]
    grad_tokens, late_sums = grad_in(
        after(tokens[0], *before), table_row, gain_one[None], in_own, in_other, grad_middle,
        list(zip(own_grads, gots)),
    )
    chains.advance(grad_tokens, (2, 3))

    shared = jnp.concatenate([late_sums[:3], sums[:4]])
    shared = shared + swap(shared, "col", 1)
    slot = lax.broadcasted_iota(jnp.int32, (seq_total, 1), 0) == seq_index
    packed = jnp.concatenate(
        [
            jnp.concatenate([shared[:2], shared[3:]]).reshape(-1),
            jnp.concatenate([part[:1] for part in bias_sums], axis=1).reshape(-1),
            jnp.concatenate([part[1:2] for part in bias_sums], axis=1).reshape(-1),
            grad_b_up,
            jnp.where(slot, shared[2:3], 0.0).reshape(-1),
            jnp.where(slot, timesteps[0].astype(wide), 0.0).reshape(-1),
        ]
    )
    pad = -packed.shape[0] % 1024
    chains.add(vector_steps(jnp.pad(packed, (0, pad)).reshape(-1, 128)))
    while not {2, 3, 4} <= set(chains.done):
        chains.advance(None, (2, 3, 4))
    chains.advance(chains.done[4])
    done = chains.done
    own_up_out, own_down = done[0], done[1]
    own_in = jnp.concatenate([done[2], done[3]], axis=1)
    own_in = [
        jnp.concatenate([own_in[:, 128 * n : 128 * (n + 1)] for n in range(kind, 3 * pairs, 3)], axis=1)
        for kind in range(3)
    ]
    packed = done[4].reshape(-1)
    place = 0
    taken = []
    for size in (6 * model_width, 2 * head_cols, hidden_cols, seq_total * model_width, seq_total):
        taken.append(packed[place : place + size])
        place += size
    six = taken[0].reshape(6, model_width)
    step_onehot = (
        lax.broadcasted_iota(jnp.int32, (seq_total, table.shape[0]), 1)
        == taken[4][:, None].astype(jnp.int32)
    ).astype(wide)
    grad_table = jnp.einsum(
        "sv,sd->vd",
        step_onehot,
        taken[3].reshape(seq_total, model_width),
        precision=lax.Precision.HIGHEST,
        preferred_element_type=wide,
    )
    return (
        layer_out[None],
        grad_tokens[None],
        grad_table,
        six[0],
        six[1],
        own_in[0],
        own_in[1],
        own_in[2],
        taken[1][:head_cols],
        taken[1][head_cols:],
        own_up_out[:, hidden_cols:].T,
        six[2],
        six[3],
        six[4],
        own_up_out[:, :hidden_cols],
        taken[2],
        own_down.T,
        six[5],
    )


def solution(mesh):
    return jax.shard_map(
        shards,
        mesh=mesh,
        in_specs=(
            P(("dp", "row"), "col", None),
            P(("dp", "row")),
            P(("dp", "row"), None),
            P(),
            P(),
            P(),
            P("row", "col"),
            P("row", "col"),
            P("row", "col"),
            P("col"),
            P("col"),
            P("col", "row"),
            P(),
            P(),
            P(),
            P("row", "col"),
            P("col"),
            P("col", "row"),
            P(),
            P(("dp", "row"), "col", None),
        ),
        out_specs=(
            P(("dp", "row"), "col", None),
            P(("dp", "row"), "col", None),
            P(),
            P(),
            P(),
            P("row", "col"),
            P("row", "col"),
            P("row", "col"),
            P("col"),
            P("col"),
            P("col", "row"),
            P(),
            P(),
            P(),
            P("row", "col"),
            P("col"),
            P("col", "row"),
            P(),
        ),
        check_vma=False,
    )
```

time: 529 us -> 442 us (0.84)
  Pallas kernels: 117 us -> 277 us
  matrix products: 116 us -> 3.12 us
  starting transfers between devices: 88.4 us -> 42.4 us
  waiting for transfers between devices: 100 us -> 66.7 us
  local copies, waits for them, and re-layouts: 52.9 us -> 20.7 us
  other arithmetic: 44.9 us -> 25.5 us
    pallas_call x0 -> x11, Pallas kernels: none -> 123 us  [the longest x1 48.5 us: feed(): pl.pallas_call(functools.partial(feed_body, layout_of(mine), head_cols, h...]
    dot_general x13 -> x0, matrix products: 113 us -> none  [the longest x3 56.1 us: dot_nn(): lax.dot_general(left, right, (((1,), (0,)), ((), ())), preferred_element_...]
    ppermute x15 -> x0, starting transfers between devices: 45.6 us -> none  [the longest x5 35.6 us: sum_line(): kept = kept + lax.ppermute(values, 'dp', [(0, 1), (3, 2)]).astype(wide)]
    ppermute x15 -> x0, waiting for transfers between devices: 44.8 us -> none  [the longest x5 24 us: sum_line(): outer = lax.ppermute(total, 'dp', [(1, 0), (2, 3)])]
    pallas_call x1 -> x3, Pallas kernels: 74.7 us -> 94.9 us  [attend_backward(): pl.pallas_call(functools.partial(attend_backward_body, count, half), grid...]
    dynamic_update_slice x20 -> x0, local copies, waits for them, and re-layouts: 19.8 us -> none  [the longest x9 10.7 us: gather_row(): whole = lax.dynamic_update_slice(whole, upper, (base, 0))]
    pallas_call x1 -> x2, Pallas kernels: 41.9 us -> 58.6 us  [attend_forward(): pl.pallas_call(functools.partial(attend_forward_body, count, half), grid_...]
    ppermute x49 -> x47, waiting for transfers between devices: 55.6 us -> 66.7 us  [swap(): return lax.ppermute(values, axis, [(i, i ^ distance) for i in range(size)])]
  transfers between devices with their start and end apart: 64 -> 47, of which waited for: 18 -> 11; matrix products, arithmetic and copies ran while one was open for 39% -> 9% of each run, Pallas kernels for 22% -> 48%
where the time goes in v2:
time: 442 us; the launch traced here: 437 us
  Pallas kernels  277 us (63%)
  waiting for transfers between devices  66.7 us (15%)
  starting transfers between devices  42.4 us (10%)
  other arithmetic  25.5 us (6%)
  local copies, waits for them, and re-layouts  20.7 us (5%)
    pallas_call x3, Pallas kernels, attend_backward(): pl.pallas_call(functools.partial(attend_backward_body, count, half), grid...  94.9 us
    ppermute x47, waiting for transfers between devices, swap(): return lax.ppermute(values, axis, [(i, i ^ distance) for i in range(size)])  66.7 us
    pallas_call x2, Pallas kernels, attend_forward(): pl.pallas_call(functools.partial(attend_forward_body, count, half), grid_...  58.6 us
    pallas_call x1, Pallas kernels, feed(): pl.pallas_call(functools.partial(feed_body, layout_of(mine), head_cols, h...  48.5 us
    ppermute x47, starting transfers between devices, swap(): return lax.ppermute(values, axis, [(i, i ^ distance) for i in range(size)])  42.4 us
    pallas_call x4, Pallas kernels, weight_parts(): pl.pallas_call(functools.partial(weight_parts_body, shapes, near), grid_s...  33 us
    pallas_call x3, Pallas kernels, product(): pl.pallas_call(product_body, grid=(columns // step,), in_specs=[pl.BlockS...  17.3 us
    pallas_call x1, Pallas kernels, grad_in(): pl.pallas_call(functools.partial(grad_in_body, cuts), grid=(rows // size,...  11.3 us
  transfers between devices with their start and end apart: 47, of which 11 were waited for; matrix products, arithmetic and copies ran while one was open for 9% of the time, Pallas kernels for 48%

profile of v2, /device:TPU:0, one launch (start us, length us, event | category | flops | bytes accessed | tf_op | source)
XLA Modules:
  0.0 437.3 jit_solution(10055845223565252327)
XLA Ops:
  0.7 2.1 pack.1.rest_0_
  2.7 2.9 collective-permute-start.2
  5.7 1.5 collective-permute-start.3
  13.1 3.0 collective-permute-done.2.rest_1_
  17.1 1.8 collective-permute-start.4
  19.9 1.6 collective-permute-start.5
  24.6 1.4 collective-permute-done.5.rest_4_
  26.7 10.8 %project_in.1 = (bf16[2,1024,1152]{2,1,0:T(8,128)(2,1)}, bf16[768,2048]{1,0:T(8,128)(2,1)}, bf16[768,1152]{1,0:T(8,128)(2,1)}) custom-call(s32[2]{0:T(128)} %pad_add_fusion.meta_ref.col_ref, bf16[1024,768]{1,0:T(8,128)(2,1)} %copy-done.1, bf16[1024,768]{1,0:T(8,128)(2,1)} %collective-permute-done.other_ref, f32[1,1152]{1,0:T(1,128)} %broadcast_in_dim.51.bias_ref, ...), custom_call_target="tpu_custom_call" | custom-call | flops 7699999744 | bytes 1048576 | tf_op jit(solution)/shard_map/project_in/pallas_call | solution.py:394
  38.9 1.4 collective-permute-start.9
  40.3 2.9 collective-permute-done.7.rest_5_
  44.3 38.5 %attend_forward.2 = (bf16[1024,256]{1,0:T(8,128)(2,1)}, bf16[1024,256]{1,0:T(8,128)(2,1)}, f32[2,2048,2]{2,1,0:T(8,128)}) custom-call(s32[2]{0:T(128)} %pad_add_fusion.meta_ref.col_ref, bf16[2,1024,1152]{2,1,0:T(8,128)(2,1)} %get-tuple-element.127.q_ref.k_ref.v_ref, bf16[2,1024,1152]{2,1,0:T(8,128)(2,1)} %get-tuple-element.127.q_ref.k_ref.v_ref, ...), custom_call_target="tpu_custom_call" | custom-call | flops 30799998976 | bytes 1048576 | tf_op jit(solution)/shard_map/attend_forward/pallas_call | solution.py:127
  84.8 1.6 collective-permute-start.15
  88.9 20.1 %attend_forward.3 = (bf16[1024,128]{1,0:T(8,128)(2,1)}, bf16[1024,128]{1,0:T(8,128)(2,1)}, f32[1,2048,2]{2,1,0:T(8,128)}) custom-call(s32[2]{0:T(128)} %pad_add_fusion.meta_ref.col_ref, bf16[2,1024,1152]{2,1,0:T(8,128)(2,1)} %get-tuple-element.127.q_ref.k_ref.v_ref, bf16[2,1024,1152]{2,1,0:T(8,128)(2,1)} %get-tuple-element.127.q_ref.k_ref.v_ref, ...), custom_call_target="tpu_custom_call" | custom-call | flops 15399999488 | bytes 1048576 | tf_op jit(solution)/shard_map/attend_forward/pallas_call | solution.py:127
  110.5 2.2 collective-permute-done.13.got_last_ref
  113.9 48.5 %feed.1 = (bf16[1024,768]{1,0:T(8,128)(2,1)}, bf16[1024,1536]{1,0:T(8,128)(2,1)}, bf16[1024,1536]{1,0:T(8,128)(2,1)}, bf16[1024,1536]{1,0:T(8,128)(2,1)}, bf16[1...) custom-call(s32[2]{0:T(128)} %pad_add_fusion.meta_ref.col_ref, ...), custom_call_target="tpu_custom_call" | custom-call | flops 49500000256 | bytes 1048576 | tf_op jit(solution)/shard_map/feed/pallas_call | solution.py:522
  162.5 6.9 %product.3 = bf16[768,1536]{1,0:T(8,128)(2,1)} custom-call(bf16[768,1024]{1,0:T(8,128)(2,1)} %get-tuple-element.98.left_ref.refs_0_, bf16[1024,1536]{1,0:T(8,128)(2,1)} %get-tuple-element.100.right_ref), custom_call_target="tpu_custom_call" | custom-call | flops 4400000000 | bytes 1048576 | tf_op jit(solution)/shard_map/product/pallas_call | solution.py:625
  169.5 6.9 %product.5 = bf16[768,1536]{1,0:T(8,128)(2,1)} custom-call(bf16[768,1024]{1,0:T(8,128)(2,1)} %get-tuple-element.104.left_ref.refs_0_, bf16[1024,1536]{1,0:T(8,128)(2,1)} %get-tuple-element.107.right_ref), custom_call_target="tpu_custom_call" | custom-call | flops 4400000000 | bytes 1048576 | tf_op jit(solution)/shard_map/product/pallas_call | solution.py:625
  177.7 3.5 product.4
  184.7 1.4 copy-done.33
  186.1 10.4 %weight_parts.4 = (bf16[384,1920]{1,0:T(8,128)(2,1)}, bf16[384,1920]{1,0:T(8,128)(2,1)}) custom-call(s32[2]{0:T(128)} %pad_add_fusion.meta_ref.col_ref, bf16[768,1024]{1,0:T(8,128)(2,1)} %get-tuple-element.98.left_ref.refs_0_, bf16[1024,1536]{1,0:T(8,128)(2,1)} %get-tuple-element.99.refs_1_, bf16[768,1536]{1,0:T(8,128)(2,1)} %copy-done.33, ...), custom_call_target="tpu_custom_call" | custom-call | flops 8800000000 | bytes 1048576 | tf_op jit(solution)/shard_map/weight_parts/pallas_call | solution.py:603
  196.5 1.5 collective-permute-start.20
  198.0 8.0 %weight_parts.5 = (bf16[384,1536]{1,0:T(8,128)(2,1)}, bf16[384,1536]{1,0:T(8,128)(2,1)}) custom-call(s32[2]{0:T(128)} %pad_add_fusion.meta_ref.col_ref, bf16[768,1024]{1,0:T(8,128)(2,1)} %get-tuple-element.104.left_ref.refs_0_, bf16[1024,1536]{1,0:T(8,128)(2,1)} %get-tuple-element.106.refs_1_, bf16[768,1536]{1,0:T(8,128)(2,1)} %collective-permute-done.21.refs_2_), custom_call_target="tpu_custom_call" | custom-call | flops 7699999744 | bytes 1048576 | tf_op jit(solution)/shard_map/weight_parts/pallas_call | solution.py:603
  207.4 31.4 %attend_backward.3 = (bf16[1024,384]{1,0:T(8,128)(2,1)}, bf16[1024,384]{1,0:T(8,128)(2,1)}, f32[8,128]{1,0:T(8,128)}) custom-call(s32[2]{0:T(128)} %pad_add_fusion.meta_ref.col_ref, bf16[2,1024,1152]{2,1,0:T(8,128)(2,1)} %get-tuple-element.127.q_ref.k_ref.v_ref, bf16[2,1024,1152]{2,1,0:T(8,128)(2,1)} %get-tuple-element.127.q_ref.k_ref.v_ref, ...), custom_call_target="tpu_custom_call" | custom-call | flops 27499999232 | bytes 1048576 | tf_op jit(solution)/shard_map/attend_backward/pallas_call | solution.py:260
  240.2 2.2 add_convert_fusion.8
  244.1 1.5 collective-permute-start.24
  245.6 31.8 %attend_backward.4 = (bf16[1024,384]{1,0:T(8,128)(2,1)}, bf16[1024,384]{1,0:T(8,128)(2,1)}, f32[8,128]{1,0:T(8,128)}) custom-call(s32[2]{0:T(128)} %pad_add_fusion.meta_ref.col_ref, bf16[2,1024,1152]{2,1,0:T(8,128)(2,1)} %get-tuple-element.127.q_ref.k_ref.v_ref, bf16[2,1024,1152]{2,1,0:T(8,128)(2,1)} %get-tuple-element.127.q_ref.k_ref.v_ref, ...), custom_call_target="tpu_custom_call" | custom-call | flops 27499999232 | bytes 1048576 | tf_op jit(solution)/shard_map/attend_backward/pallas_call | solution.py:260
  277.5 9.2 %weight_parts.6 = (bf16[384,768]{1,0:T(8,128)(2,1)}, bf16[384,768]{1,0:T(8,128)(2,1)}) custom-call(s32[2]{0:T(128)} %pad_add_fusion.meta_ref.col_ref, bf16[768,2048]{1,0:T(8,128)(2,1)} %get-tuple-element.124.refs_0_.refs_2_.refs_4_.refs_6_, bf16[1024,384]{1,0:T(8,128)(2,1)} %get-tuple-element.115.refs_1_.rest_0_, ...), custom_call_target="tpu_custom_call" | custom-call | flops 6600000000 | bytes 1048576 | tf_op jit(solution)/shard_map/weight_parts/pallas_call | solution.py:603
  288.6 1.5 add_convert_fusion.7
  290.1 1.6 collective-permute-start.30
  291.7 1.4 add_convert_fusion.3
  293.7 31.7 %attend_backward.5 = (bf16[1024,384]{1,0:T(8,128)(2,1)}, bf16[1024,384]{1,0:T(8,128)(2,1)}, f32[8,128]{1,0:T(8,128)}) custom-call(s32[2]{0:T(128)} %pad_add_fusion.meta_ref.col_ref, bf16[2,1024,1152]{2,1,0:T(8,128)(2,1)} %get-tuple-element.127.q_ref.k_ref.v_ref, bf16[2,1024,1152]{2,1,0:T(8,128)(2,1)} %get-tuple-element.127.q_ref.k_ref.v_ref, ...), custom_call_target="tpu_custom_call" | custom-call | flops 27499999232 | bytes 1048576 | tf_op jit(solution)/shard_map/attend_backward/pallas_call | solution.py:260
  325.5 1.7 add_convert_fusion.12
  327.2 1.5 collective-permute-start.38
  328.7 5.5 %weight_parts.7 = (bf16[384,384]{1,0:T(8,128)(2,1)}, bf16[384,384]{1,0:T(8,128)(2,1)}) custom-call(s32[2]{0:T(128)} %pad_add_fusion.meta_ref.col_ref, bf16[768,2048]{1,0:T(8,128)(2,1)} %get-tuple-element.124.refs_0_.refs_2_.refs_4_.refs_6_, bf16[1024,384]{1,0:T(8,128)(2,1)} %get-tuple-element.129.refs_1_.rest_4_, ...), custom_call_target="tpu_custom_call" | custom-call | flops 3300000000 | bytes 1048576 | tf_op jit(solution)/shard_map/weight_parts/pallas_call | solution.py:603
  336.2 11.3 %grad_in.1 = (f32[1024,768]{1,0:T(8,128)}, f32[8,768]{1,0:T(8,128)}) custom-call(bf16[1024,768]{1,0:T(8,128)(2,1)} %bitcast.50, f32[1,768]{1,0:T(1,128)} %get-tuple-element.151.row_ref, f32[1,768]{1,0:T(1,128)} %broadcast_in_dim.53.gain_ref, bf16[768,1152]{1,0:T(8,128)(2,1)} %get-tuple-element.85.own_ref, ...), custom_call_target="tpu_custom_call" | custom-call | flops 9900000256 | bytes 1048576 | tf_op jit(solution)/shard_map/grad_in/pallas_call | solution.py:692
  349.1 2.6 collective-permute-start.46
  352.4 1.5 collective-permute-start.34
  355.1 1.6 collective-permute-start.39
  356.9 1.5 collective-permute-start.35
  360.0 1.7 collective-permute-done.35
  361.7 1.9 collective-permute-start.36
  365.6 1.6 collective-permute-start.43
  367.2 22.0 %collective-permute-done.36 = f32[152,128]{1,0:T(8,128)S(1)} collective-permute-done((f32[152,128]{1,0:T(8,128)S(1)}, f32[152,128]{1,0:T(8,128)S(1)}, u32[]{:S(2)}, u32[]{:S(2)}) %collective-permute-start.36) | collective-permute-done | bytes 77856 | tf_op jit(solution)/shard_map/ppermute | solution.py:328
  389.2 2.5 collective-permute-start.37
  392.4 2.5 collective-permute-start.44
  394.9 28.4 %collective-permute-done.37 = f32[152,128]{1,0:T(8,128)S(1)} collective-permute-done((f32[152,128]{1,0:T(8,128)S(1)}, f32[152,128]{1,0:T(8,128)S(1)}, u32[]{:S(2)}, u32[]{:S(2)}) %collective-permute-start.37) | collective-permute-done | bytes 77856 | tf_op jit(solution)/shard_map/ppermute | solution.py:328
  425.7 3.1 fusion.5
  429.4 2.9 collective-permute-done.44
  (243 shorter events, 50.0 us)
Async XLA Ops:
  2.7 13.4 %collective-permute-start.2 = (bf16[192,1152]{1,0:T(8,128)(2,1)}, bf16[192,1152]{1,0:T(8,128)(2,1)}, u32[]{:S(2)}, u32[]{:S(2)}) collective-permute-start(bf16[192,1152]{1,0:T(8,128)(2,1)} %pack.1.rest_0_), channel_id=1, source_target_pairs={{0,2},{2,0},{4,6},{6,4},{1,3},{3,1},{5,7},{7,5},{8,10},{10,8},{12,... | collective-permute-start | bytes 1327112 | tf_op jit(solution)/shard_map/ppermute | solution.py:328
  5.7 13.3 %collective-permute-start.3 = (bf16[192,1152]{1,0:T(8,128)(2,1)}, bf16[192,1152]{1,0:T(8,128)(2,1)}, u32[]{:S(2)}, u32[]{:S(2)}) collective-permute-start(bf16[192,1152]{1,0:T(8,128)(2,1)} %pack.1.rest_0_), channel_id=1, source_target_pairs={{0,4},{2,6},{4,0},{6,2},{1,5},{3,7},{5,1},{7,3},{8,12},{10,14},{12... | collective-permute-start | bytes 1327112 | tf_op jit(solution)/shard_map/ppermute | solution.py:328
  11.1 13.6 %collective-permute-start = (bf16[1024,768]{1,0:T(8,128)(2,1)S(1)}, bf16[1024,768]{1,0:T(8,128)(2,1)}, u32[]{:S(2)}, u32[]{:S(2)}) collective-permute-start(bf16[1024,768]{1,0:T(8,128)(2,1)S(1)} %add_convert_fusion.mine_ref), channel_id=1, source_target_pairs={{0,1},{1,0},{2,3},{3,2},{4,5},{5,4},{6,7},{7,6},{8,9},{9,8},{10,11... | collective-permute-start | bytes 4718600 | tf_op jit(solution)/shard_map/ppermute | solution.py:328
  11.1 12.8 %collective-permute-start.1 = (f32[1536]{0:T(1024)S(1)}, f32[1536]{0:T(1024)S(1)}, u32[]{:S(2)}, u32[]{:S(2)}) collective-permute-start(f32[1536]{0:T(1024)S(1)} %copy-done.22), channel_id=1, source_target_pairs={{0,1},{1,0},{2,3},{3,2},{4,5},{5,4},{6,7},{7,6},{8,9},{9,8},{10,11... | collective-permute-start | bytes 18440 | tf_op jit(solution)/shard_map/ppermute | solution.py:328
  17.1 7.5 %collective-permute-start.4 = (bf16[96,1152]{1,0:T(8,128)(2,1)S(1)}, bf16[96,1152]{1,0:T(8,128)(2,1)S(1)}, u32[]{:S(2)}, u32[]{:S(2)}) collective-permute-start(bf16[96,1152]{1,0:T(8,128)(2,1)S(1)} %slice.275), channel_id=1, source_target_pairs={{0,4},{2,6},{4,0},{6,2},{1,5},{3,7},{5,1},{7,3},{8,12},{10,14},{12... | collective-permute-start | bytes 663560 | tf_op jit(solution)/shard_map/ppermute | solution.py:328
  19.9 6.1 %collective-permute-start.5 = (bf16[96,1152]{1,0:T(8,128)(2,1)S(1)}, bf16[96,1152]{1,0:T(8,128)(2,1)S(1)}, u32[]{:S(2)}, u32[]{:S(2)}) collective-permute-start(bf16[96,1152]{1,0:T(8,128)(2,1)S(1)} %slice.276), channel_id=1, source_target_pairs={{0,2},{2,0},{4,6},{6,4},{1,3},{3,1},{5,7},{7,5},{8,10},{10,8},{12,... | collective-permute-start | bytes 663560 | tf_op jit(solution)/shard_map/ppermute | solution.py:328
  37.5 6.7 %collective-permute-start.6 = (bf16[768,1152]{1,0:T(8,128)(2,1)}, bf16[768,1152]{1,0:T(8,128)(2,1)}, u32[]{:S(2)}, u32[]{:S(2)}) collective-permute-start(bf16[768,1152]{1,0:T(8,128)(2,1)} %get-tuple-element.85.own_ref), channel_id=1, source_target_pairs={{0,1},{1,0},{2,3},{3,2},{4,5},{5,4},{6,7},{7,6},{8,9},{9,8},{10,11... | collective-permute-start | bytes 5308424 | tf_op jit(solution)/shard_map/ppermute | solution.py:328
  37.7 45.1 %copy-start.5 = (bf16[192,3456]{1,0:T(8,128)(2,1)}, bf16[192,3456]{1,0:T(8,128)(2,1)S(1)}, u32[]{:S(2)}) copy-start(bf16[192,3456]{1,0:T(8,128)(2,1)S(1)} %pad_maximum_fusion.rest_0_) | copy-start | bytes 3981316
  37.7 5.5 %collective-permute-start.7 = (bf16[192,3456]{1,0:T(8,128)(2,1)S(1)}, bf16[192,3456]{1,0:T(8,128)(2,1)S(1)}, u32[]{:S(2)}, u32[]{:S(2)}) collective-permute-start(bf16[192,3456]{1,0:T(8,128)(2,1)S(1)} %pad_maximum_fusion.rest_0_), channel_id=1, source_target_pairs={{0,1},{1,0},{2,3},{3,2},{4,5},{5,4},{6,7},{7,6},{8,9},{9,8},{10,11... | collective-permute-start | bytes 3981320 | tf_op jit(solution)/shard_map/ppermute | solution.py:328
  38.3 44.5 %collective-permute-start.11 = (bf16[192,3456]{1,0:T(8,128)(2,1)S(1)}, bf16[192,3456]{1,0:T(8,128)(2,1)S(1)}, u32[]{:S(2)}, u32[]{:S(2)}) collective-permute-start(bf16[192,3456]{1,0:T(8,128)(2,1)S(1)} %pad_maximum_fusion.rest_0_), channel_id=1, source_target_pairs={{0,4},{2,6},{4,0},{6,2},{1,5},{3,7},{5,1},{7,3},{8,12},{10,14},{12... | collective-permute-start | bytes 3981320 | tf_op jit(solution)/shard_map/ppermute | solution.py:328
  38.9 44.2 %collective-permute-start.9 = (bf16[192,3456]{1,0:T(8,128)(2,1)S(1)}, bf16[192,3456]{1,0:T(8,128)(2,1)}, u32[]{:S(2)}, u32[]{:S(2)}) collective-permute-start(bf16[192,3456]{1,0:T(8,128)(2,1)S(1)} %pad_maximum_fusion.rest_0_), channel_id=1, source_target_pairs={{0,2},{2,0},{4,6},{6,4},{1,3},{3,1},{5,7},{7,5},{8,10},{10,8},{12,... | collective-permute-start | bytes 3981320 | tf_op jit(solution)/shard_map/ppermute | solution.py:328
  82.8 5.0 %collective-permute-start.12 = (bf16[192,3456]{1,0:T(8,128)(2,1)S(1)}, bf16[192,3456]{1,0:T(8,128)(2,1)S(1)}, u32[]{:S(2)}, u32[]{:S(2)}) collective-permute-start(bf16[192,3456]{1,0:T(8,128)(2,1)S(1)} %collective-permute-done.11.rest_2_), channel_id=1, source_target_pairs={{0,1},{1,0},{2,3},{3,2},{4,5},{5,4},{6,7},{7,6},{8,9},{9,8},{10,11... | collective-permute-start | bytes 3981320 | tf_op jit(solution)/shard_map/ppermute | solution.py:328
  83.0 5.9 %collective-permute-start.10 = (bf16[192,3456]{1,0:T(8,128)(2,1)}, bf16[192,3456]{1,0:T(8,128)(2,1)}, u32[]{:S(2)}, u32[]{:S(2)}) collective-permute-start(bf16[192,3456]{1,0:T(8,128)(2,1)} %collective-permute-done.9.rest_1_), channel_id=1, source_target_pairs={{0,1},{1,0},{2,3},{3,2},{4,5},{5,4},{6,7},{7,6},{8,9},{9,8},{10,11... | collective-permute-start | bytes 3981320 | tf_op jit(solution)/shard_map/ppermute | solution.py:328
  83.4 4.4 %collective-permute-start.8 = (bf16[1024,256]{1,0:T(8,128)(2,1)}, bf16[1024,256]{1,0:T(8,128)(2,1)S(1)}, u32[]{:S(2)}, u32[]{:S(2)}) collective-permute-start(bf16[1024,256]{1,0:T(8,128)(2,1)} %get-tuple-element.89), channel_id=1, source_target_pairs={{0,1},{1,0},{2,3},{3,2},{4,5},{5,4},{6,7},{7,6},{8,9},{9,8},{10,11... | collective-permute-start | bytes 1572872 | tf_op jit(solution)/shard_map/ppermute | solution.py:328
  84.8 24.3 %collective-permute-start.15 = (bf16[96,3456]{1,0:T(8,128)(2,1)S(1)}, bf16[96,3456]{1,0:T(8,128)(2,1)}, u32[]{:S(2)}, u32[]{:S(2)}) collective-permute-start(bf16[96,3456]{1,0:T(8,128)(2,1)S(1)} %slice.220), channel_id=1, source_target_pairs={{0,2},{2,0},{4,6},{6,4},{1,3},{3,1},{5,7},{7,5},{8,10},{10,8},{12,... | collective-permute-start | bytes 1990664 | tf_op jit(solution)/shard_map/ppermute | solution.py:328
  86.3 23.0 %collective-permute-start.14 = (bf16[96,3456]{1,0:T(8,128)(2,1)S(1)}, bf16[96,3456]{1,0:T(8,128)(2,1)}, u32[]{:S(2)}, u32[]{:S(2)}) collective-permute-start(bf16[96,3456]{1,0:T(8,128)(2,1)S(1)} %slice.219), channel_id=1, source_target_pairs={{0,4},{2,6},{4,0},{6,2},{1,5},{3,7},{5,1},{7,3},{8,12},{10,14},{12... | collective-permute-start | bytes 1990664 | tf_op jit(solution)/shard_map/ppermute | solution.py:328
  109.1 3.7 collective-permute-start.17
  109.3 3.5 collective-permute-start.16
  109.6 3.1 collective-permute-start.13
  169.3 15.4 %collective-permute-start.18 = (bf16[768,1536]{1,0:T(8,128)(2,1)}, bf16[768,1536]{1,0:T(8,128)(2,1)S(1)}, u32[]{:S(2)}, u32[]{:S(2)}) collective-permute-start(bf16[768,1536]{1,0:T(8,128)(2,1)} %product.3), channel_id=1, source_target_pairs={{0,1},{1,0},{2,3},{3,2},{4,5},{5,4},{6,7},{7,6},{8,9},{9,8},{10,11... | collective-permute-start | bytes 7077896 | tf_op jit(solution)/shard_map/ppermute | solution.py:328
  176.4 21.5 %collective-permute-start.21 = (bf16[768,1536]{1,0:T(8,128)(2,1)}, bf16[768,1536]{1,0:T(8,128)(2,1)}, u32[]{:S(2)}, u32[]{:S(2)}) collective-permute-start(bf16[768,1536]{1,0:T(8,128)(2,1)} %product.5), channel_id=1, source_target_pairs={{0,1},{1,0},{2,3},{3,2},{4,5},{5,4},{6,7},{7,6},{8,9},{9,8},{10,11... | collective-permute-start | bytes 7077896 | tf_op jit(solution)/shard_map/ppermute | solution.py:328
  181.2 3.5 collective-permute-start.19
  182.5 1.5 collective-permute-start.22
  183.9 22.6 %collective-permute-start.23 = (bf16[1024,384]{1,0:T(8,128)(2,1)}, bf16[1024,384]{1,0:T(8,128)(2,1)S(1)}, u32[]{:S(2)}, u32[]{:S(2)}) collective-permute-start(bf16[1024,384]{1,0:T(8,128)(2,1)} %get-tuple-element.113), channel_id=1, source_target_pairs={{0,1},{1,0},{2,3},{3,2},{4,5},{5,4},{6,7},{7,6},{8,9},{9,8},{10,11... | collective-permute-start | bytes 2359304 | tf_op jit(solution)/shard_map/ppermute | solution.py:328
  196.5 46.5 %collective-permute-start.20 = (bf16[384,1920]{1,0:T(8,128)(2,1)}, bf16[384,1920]{1,0:T(8,128)(2,1)S(1)}, u32[]{:S(2)}, u32[]{:S(2)}) collective-permute-start(bf16[384,1920]{1,0:T(8,128)(2,1)} %get-tuple-element.103), channel_id=1, source_target_pairs={{0,2},{2,0},{4,6},{6,4},{1,3},{3,1},{5,7},{7,5},{8,10},{10,8},{12,... | collective-permute-start | bytes 4423688 | tf_op jit(solution)/shard_map/ppermute | solution.py:328
  205.9 34.2 %collective-permute-start.25 = (bf16[384,1536]{1,0:T(8,128)(2,1)}, bf16[384,1536]{1,0:T(8,128)(2,1)}, u32[]{:S(2)}, u32[]{:S(2)}) collective-permute-start(bf16[384,1536]{1,0:T(8,128)(2,1)} %get-tuple-element.108), channel_id=1, source_target_pairs={{0,4},{2,6},{4,0},{6,2},{1,5},{3,7},{5,1},{7,3},{8,12},{10,14},{12... | collective-permute-start | bytes 3538952 | tf_op jit(solution)/shard_map/ppermute | solution.py:328
  238.8 6.8 %collective-permute-start.26 = (bf16[1024,384]{1,0:T(8,128)(2,1)}, bf16[1024,384]{1,0:T(8,128)(2,1)}, u32[]{:S(2)}, u32[]{:S(2)}) collective-permute-start(bf16[1024,384]{1,0:T(8,128)(2,1)} %get-tuple-element.118.refs_3_), channel_id=1, source_target_pairs={{0,1},{1,0},{2,3},{3,2},{4,5},{5,4},{6,7},{7,6},{8,9},{9,8},{10,11... | collective-permute-start | bytes 2359304 | tf_op jit(solution)/shard_map/ppermute | solution.py:328
  242.4 46.3 %collective-permute-start.28 = (bf16[192,1536]{1,0:T(8,128)(2,1)}, bf16[192,1536]{1,0:T(8,128)(2,1)}, u32[]{:S(2)}, u32[]{:S(2)}) collective-permute-start(bf16[192,1536]{1,0:T(8,128)(2,1)} %add_convert_fusion.8), channel_id=1, source_target_pairs={{0,2},{2,0},{4,6},{6,4},{1,3},{3,1},{5,7},{7,5},{8,10},{10,8},{12,... | collective-permute-start | bytes 1769480 | tf_op jit(solution)/shard_map/ppermute | solution.py:328
  244.1 47.6 %collective-permute-start.24 = (bf16[192,1920]{1,0:T(8,128)(2,1)}, bf16[192,1920]{1,0:T(8,128)(2,1)}, u32[]{:S(2)}, u32[]{:S(2)}) collective-permute-start(bf16[192,1920]{1,0:T(8,128)(2,1)} %add_convert_fusion.4), channel_id=1, source_target_pairs={{0,4},{2,6},{4,0},{6,2},{1,5},{3,7},{5,1},{7,3},{8,12},{10,14},{12... | collective-permute-start | bytes 2211848 | tf_op jit(solution)/shard_map/ppermute | solution.py:328
  277.4 16.2 %collective-permute-start.29 = (bf16[1024,384]{1,0:T(8,128)(2,1)}, bf16[1024,384]{1,0:T(8,128)(2,1)}, u32[]{:S(2)}, u32[]{:S(2)}) collective-permute-start(bf16[1024,384]{1,0:T(8,128)(2,1)} %get-tuple-element.123.refs_7_), channel_id=1, source_target_pairs={{0,1},{1,0},{2,3},{3,2},{4,5},{5,4},{6,7},{7,6},{8,9},{9,8},{10,11... | collective-permute-start | bytes 2359304 | tf_op jit(solution)/shard_map/ppermute | solution.py:328
  286.7 38.7 %collective-permute-start.31 = (bf16[384,768]{1,0:T(8,128)(2,1)}, bf16[384,768]{1,0:T(8,128)(2,1)}, u32[]{:S(2)}, u32[]{:S(2)}) collective-permute-start(bf16[384,768]{1,0:T(8,128)(2,1)} %get-tuple-element.125), channel_id=1, source_target_pairs={{0,4},{2,6},{4,0},{6,2},{1,5},{3,7},{5,1},{7,3},{8,12},{10,14},{12... | collective-permute-start | bytes 1769480 | tf_op jit(solution)/shard_map/ppermute | solution.py:328
  290.1 44.6 %collective-permute-start.30 = (bf16[192,1536]{1,0:T(8,128)(2,1)S(1)}, bf16[192,1536]{1,0:T(8,128)(2,1)}, u32[]{:S(2)}, u32[]{:S(2)}) collective-permute-start(bf16[192,1536]{1,0:T(8,128)(2,1)S(1)} %add_convert_fusion.7), channel_id=1, source_target_pairs={{0,8},{8,0},{16,24},{24,16},{1,9},{9,1},{17,25},{25,17},{2,10},{10... | collective-permute-start | bytes 1769480 | tf_op jit(solution)/shard_map/ppermute | solution.py:328
  293.1 42.8 %collective-permute-start.27 = (bf16[192,1920]{1,0:T(8,128)(2,1)S(1)}, bf16[192,1920]{1,0:T(8,128)(2,1)S(1)}, u32[]{:S(2)}, u32[]{:S(2)}) collective-permute-start(bf16[192,1920]{1,0:T(8,128)(2,1)S(1)} %add_convert_fusion.3), channel_id=1, source_target_pairs={{0,8},{8,0},{16,24},{24,16},{1,9},{9,1},{17,25},{25,17},{2,10},{10... | collective-permute-start | bytes 2211848 | tf_op jit(solution)/shard_map/ppermute | solution.py:328
  325.4 10.7 %collective-permute-start.32 = (bf16[1024,384]{1,0:T(8,128)(2,1)}, bf16[1024,384]{1,0:T(8,128)(2,1)}, u32[]{:S(2)}, u32[]{:S(2)}) collective-permute-start(bf16[1024,384]{1,0:T(8,128)(2,1)} %get-tuple-element.133.refs_3_), channel_id=1, source_target_pairs={{0,1},{1,0},{2,3},{3,2},{4,5},{5,4},{6,7},{7,6},{8,9},{9,8},{10,11... | collective-permute-start | bytes 2359304 | tf_op jit(solution)/shard_map/ppermute | solution.py:328
  327.2 24.9 %collective-permute-start.38 = (bf16[192,768]{1,0:T(8,128)(2,1)}, bf16[192,768]{1,0:T(8,128)(2,1)}, u32[]{:S(2)}, u32[]{:S(2)}) collective-permute-start(bf16[192,768]{1,0:T(8,128)(2,1)} %add_convert_fusion.12), channel_id=1, source_target_pairs={{0,2},{2,0},{4,6},{6,4},{1,3},{3,1},{5,7},{7,5},{8,10},{10,8},{12,... | collective-permute-start | bytes 884744 | tf_op jit(solution)/shard_map/ppermute | solution.py:328
  334.2 22.6 %collective-permute-start.41 = (bf16[384,384]{1,0:T(8,128)(2,1)}, bf16[384,384]{1,0:T(8,128)(2,1)}, u32[]{:S(2)}, u32[]{:S(2)}) collective-permute-start(bf16[384,384]{1,0:T(8,128)(2,1)} %get-tuple-element.134), channel_id=1, source_target_pairs={{0,2},{2,0},{4,6},{6,4},{1,3},{3,1},{5,7},{7,5},{8,10},{10,8},{12,... | collective-permute-start | bytes 884744 | tf_op jit(solution)/shard_map/ppermute | solution.py:328
  348.2 3.9 collective-permute-start.33
  349.1 75.4 %collective-permute-start.46 = (bf16[192,1536]{1,0:T(8,128)(2,1)S(1)}, bf16[192,1536]{1,0:T(8,128)(2,1)S(1)}, u32[]{:S(2)}, u32[]{:S(2)}) collective-permute-start(bf16[192,1536]{1,0:T(8,128)(2,1)S(1)} %add_convert_fusion.6), channel_id=1, source_target_pairs={{0,16},{8,24},{16,0},{24,8},{1,17},{9,25},{17,1},{25,9},{2,18},{10... | collective-permute-start | bytes 1769480 | tf_op jit(solution)/shard_map/ppermute | solution.py:328
  351.7 83.4 %collective-permute-start.45 = (bf16[192,1920]{1,0:T(8,128)(2,1)S(1)}, bf16[192,1920]{1,0:T(8,128)(2,1)S(1)}, u32[]{:S(2)}, u32[]{:S(2)}) collective-permute-start(bf16[192,1920]{1,0:T(8,128)(2,1)S(1)} %add_convert_fusion.2), channel_id=1, source_target_pairs={{0,16},{8,24},{16,0},{24,8},{1,17},{9,25},{17,1},{25,9},{2,18},{10... | collective-permute-start | bytes 2211848 | tf_op jit(solution)/shard_map/ppermute | solution.py:328
  352.4 4.5 %collective-permute-start.34 = (f32[152,128]{1,0:T(8,128)S(1)}, f32[152,128]{1,0:T(8,128)S(1)}, u32[]{:S(2)}, u32[]{:S(2)}) collective-permute-start(f32[152,128]{1,0:T(8,128)S(1)} %pad_bitcast_fusion), channel_id=1, source_target_pairs={{0,2},{2,0},{4,6},{6,4},{1,3},{3,1},{5,7},{7,5},{8,10},{10,8},{12,... | collective-permute-start | bytes 233480 | tf_op jit(solution)/shard_map/ppermute | solution.py:328
  355.1 36.5 %collective-permute-start.39 = (bf16[192,768]{1,0:T(8,128)(2,1)S(1)}, bf16[192,768]{1,0:T(8,128)(2,1)S(1)}, u32[]{:S(2)}, u32[]{:S(2)}) collective-permute-start(bf16[192,768]{1,0:T(8,128)(2,1)S(1)} %add_convert_fusion.11), channel_id=1, source_target_pairs={{0,8},{8,0},{16,24},{24,16},{1,9},{9,1},{17,25},{25,17},{2,10},{10... | collective-permute-start | bytes 884744 | tf_op jit(solution)/shard_map/ppermute | solution.py:328
  356.9 4.8 %collective-permute-start.35 = (f32[152,128]{1,0:T(8,128)S(1)}, f32[152,128]{1,0:T(8,128)S(1)}, u32[]{:S(2)}, u32[]{:S(2)}) collective-permute-start(f32[152,128]{1,0:T(8,128)S(1)} %fusion.8), channel_id=1, source_target_pairs={{0,4},{2,6},{4,0},{6,2},{1,5},{3,7},{5,1},{7,3},{8,12},{10,14},{12... | collective-permute-start | bytes 233480 | tf_op jit(solution)/shard_map/ppermute | solution.py:328
  359.4 5.2 %collective-permute-start.42 = (bf16[192,384]{1,0:T(8,128)(2,1)S(1)}, bf16[192,384]{1,0:T(8,128)(2,1)S(1)}, u32[]{:S(2)}, u32[]{:S(2)}) collective-permute-start(bf16[192,384]{1,0:T(8,128)(2,1)S(1)} %add_convert_fusion.16), channel_id=1, source_target_pairs={{0,4},{2,6},{4,0},{6,2},{1,5},{3,7},{5,1},{7,3},{8,12},{10,14},{12... | collective-permute-start | bytes 442376 | tf_op jit(solution)/shard_map/ppermute | solution.py:328
  361.7 27.4 %collective-permute-start.36 = (f32[152,128]{1,0:T(8,128)S(1)}, f32[152,128]{1,0:T(8,128)S(1)}, u32[]{:S(2)}, u32[]{:S(2)}) collective-permute-start(f32[152,128]{1,0:T(8,128)S(1)} %fusion.16), channel_id=1, source_target_pairs={{0,8},{8,0},{16,24},{24,16},{1,9},{9,1},{17,25},{25,17},{2,10},{10... | collective-permute-start | bytes 233480 | tf_op jit(solution)/shard_map/ppermute | solution.py:328
  365.6 26.7 %collective-permute-start.43 = (bf16[192,384]{1,0:T(8,128)(2,1)S(1)}, bf16[192,384]{1,0:T(8,128)(2,1)S(1)}, u32[]{:S(2)}, u32[]{:S(2)}) collective-permute-start(bf16[192,384]{1,0:T(8,128)(2,1)S(1)} %add_convert_fusion.15), channel_id=1, source_target_pairs={{0,8},{8,0},{16,24},{24,16},{1,9},{9,1},{17,25},{25,17},{2,10},{10... | collective-permute-start | bytes 442376 | tf_op jit(solution)/shard_map/ppermute | solution.py:328
  389.2 34.0 %collective-permute-start.37 = (f32[152,128]{1,0:T(8,128)S(1)}, f32[152,128]{1,0:T(8,128)S(1)}, u32[]{:S(2)}, u32[]{:S(2)}) collective-permute-start(f32[152,128]{1,0:T(8,128)S(1)} %add.137), channel_id=1, source_target_pairs={{0,16},{8,24},{16,0},{24,8},{1,17},{9,25},{17,1},{25,9},{2,18},{10... | collective-permute-start | bytes 233480 | tf_op jit(solution)/shard_map/ppermute | solution.py:328
  391.8 40.6 %collective-permute-start.40 = (bf16[192,768]{1,0:T(8,128)(2,1)S(1)}, bf16[192,768]{1,0:T(8,128)(2,1)}, u32[]{:S(2)}, u32[]{:S(2)}) collective-permute-start(bf16[192,768]{1,0:T(8,128)(2,1)S(1)} %add_convert_fusion.10), channel_id=1, source_target_pairs={{0,16},{8,24},{16,0},{24,8},{1,17},{9,25},{17,1},{25,9},{2,18},{10... | collective-permute-start | bytes 884744 | tf_op jit(solution)/shard_map/ppermute | solution.py:328
  392.4 39.9 %collective-permute-start.44 = (bf16[192,384]{1,0:T(8,128)(2,1)S(1)}, bf16[192,384]{1,0:T(8,128)(2,1)S(1)}, u32[]{:S(2)}, u32[]{:S(2)}) collective-permute-start(bf16[192,384]{1,0:T(8,128)(2,1)S(1)} %add_convert_fusion.14), channel_id=1, source_target_pairs={{0,16},{8,24},{16,0},{24,8},{1,17},{9,25},{17,1},{25,9},{2,18},{10... | collective-permute-start | bytes 442376 | tf_op jit(solution)/shard_map/ppermute | solution.py:328
  (42 other events, 414.5 us)
